TPU v7x, 32 devices: a whole 2x2x4 slice. The times are simulated.
32 devices in a mesh: section: 8 (over y, x, core), replica: 4 (over z).
Axes of the slice: x: 2, y: 2, z: 4, core: 2. Of those that a mesh axis runs over, the one named last changes fastest.
Arguments:
- saved: bfloat16 [8, 2, 4, 4096, 128], P('section', None, 'replica'), may hold values from -6 to 6
- upstream: bfloat16 [8, 4, 4096, 128], P('section', 'replica'), may hold values from -0.59765625 to 0.59765625
- short_filters: float32 [8, 3, 256, 7], P('section'), may hold values from -2 to 2
- medium_filter: float32 [8, 256, 128], P('section'), may hold values from -0.5 to 0.5
- skip: float32 [8, 4096], P('section'), may hold values from -4 to 4
Outputs:
- short_grad: float32 [8, 3, 256, 7], P('section')
- medium_grad: float32 [8, 256, 128], P('section')
- skip_grad: float32 [8, 4096], P('section')
All inputs are finite; a program needn't handle non-finite values.
Results may differ from a plain program's by a relative error of at most 0.0056.
Values may be sent and summed in bfloat16 or wider, within the bound.
No kernel may reach another device: no remote copies, remote signals or barrier semaphores. Data moves between devices by JAX's collectives and lax.ppermute only.
A program may use at most 192 MiB of HBM per device.

v0:
```python
import functools

import jax
import jax.numpy as jnp
import numpy as np
from jax import lax
from jax.experimental import pallas as pl
from jax.experimental.pallas import tpu as pltpu
from jax.sharding import PartitionSpec as P

GROUP = 16
LANES = 128
SUB = 128

F32 = jnp.float32
BF16 = jnp.bfloat16
PRECISE = lax.Precision.HIGHEST


def shifted(array, axis, by):
    count = lax.axis_size(axis)
    pairs = [(i, i + by) for i in range(count) if 0 <= i + by < count]
    return lax.ppermute(array, axis, pairs)


def split(matrix):
    high = matrix.astype(jnp.bfloat16)
    low = (matrix - high.astype(np.float64)).astype(jnp.bfloat16)
    return high, low


@functools.lru_cache(None)
def tables(length, taps):
    points = 2 * length
    pos = np.arange(length)[:, None]
    freq = np.arange(length)[None, :]
    angle = 2.0 * np.pi * ((pos * freq) % points) / points
    real, imag = np.cos(angle), -np.sin(angle)
    imag[:, 0] = 1.0 - 2.0 * (np.arange(length) % 2)
    forward = np.concatenate([real, imag], axis=1)
    weight = np.full((2 * length, 1), 2.0 / points)
    weight[0] = weight[length] = 1.0 / points
    inverse = weight * forward.T
    shift = np.concatenate([np.eye(length, k=lag) for lag in range(1, taps)], axis=1)
    unshift = np.concatenate([np.eye(length, k=-lag) for lag in range(taps)], axis=0)
    return (
        np.concatenate(split(forward), axis=0),
        np.concatenate(split(inverse), axis=0),
        inverse.astype(np.float32),
        shift.astype(jnp.bfloat16),
        unshift.astype(jnp.bfloat16),
    )


def nt(left, right, precision=None):
    return lax.dot_general(
        left, right, (((1,), (1,)), ((), ())), precision=precision, preferred_element_type=F32
    )


def mm(left, right, precision=None):
    return jnp.dot(left, right, precision=precision, preferred_element_type=F32)


def row(ref, *index):
    return jnp.broadcast_to(ref[index], (GROUP, LANES))


def tick_kernel(last, taps, *refs):
    if last:
        (x_ref, cot_ref, f_ref, med_ref, skip_ref, fwd_ref, inv_ref, shift_ref, finv_ref,
         acc_in, skip_in, msg_ref, fsp, coef, xs, feat, hat, res, red, acc, skips) = refs
    else:
        (x_ref, cot_ref, f_ref, med_ref, skip_ref, fwd_ref, inv_ref, shift_ref, unshift_ref,
         gin_ref, acc, skips, fsp, coef, xs, feat, hat, res, red) = refs
    channels = x_ref.shape[-2]
    groups = channels // GROUP
    ng = SUB // GROUP
    lane = lax.broadcasted_iota(jnp.int32, (1, LANES), 1)
    first = lane == 0

    h = med_ref[0].astype(BF16)
    hh = mm(jnp.concatenate([h, h], axis=1), fwd_ref[...])
    hr, hi = hh[:, :LANES], hh[:, LANES:]
    coef[0] = hr
    coef[1] = jnp.where(first, 0.0, hi)
    coef[2] = jnp.where(first, hi, hr)

    def block(index, _):
        base = pl.multiple_of(index * SUB, SUB)
        gbase = pl.multiple_of(index * ng, ng)
        rows = pl.ds(base, SUB)
        own = lax.rem(lax.broadcasted_iota(jnp.int32, (GROUP, LANES), 1), GROUP) == (
            lax.broadcasted_iota(jnp.int32, (GROUP, LANES), 0)
        )
        x = x_ref[0, 0, 0, rows, :]
        xs[:, LANES:] = mm(x, shift_ref[...])
        xs[:, :LANES] = x.astype(F32)
        for m in range(3):
            taps_m = f_ref[0, m, pl.ds(gbase, ng), :]
            for j in range(taps):
                fsp[m * taps + j] = jnp.broadcast_to(taps_m[:, j : j + 1], (ng, LANES))
        local = [coef[i, pl.ds(gbase, ng), :] for i in range(3)]
        for i in range(3):
            red[i, :ng, :] = local[i]
        skip_cols = jnp.broadcast_to(skip_ref[pl.ds(index, 1), :], (SUB, LANES)).T

        lows, grads = [], []
        for k in range(ng):
            r = slice(GROUP * k, GROUP * (k + 1))
            f = [None] * 3
            for m in range(3):
                total = None
                for j in range(taps):
                    term = row(fsp, m * taps + j, slice(k, k + 1)) * xs[r, LANES * j : LANES * (j + 1)]
                    total = term if total is None else total + term
                f[m] = total
            product = f[1] * f[2]
            cot = cot_ref[pl.ds(base + GROUP * k, GROUP), :].astype(F32)
            gm = cot * f[0]
            feat[0, r] = f[1]
            feat[1, r] = f[2]
            feat[2, r] = product
            feat[3, r] = gm
            lows.append(product.astype(BF16))
            grads.append(gm.astype(BF16))
        both = jnp.concatenate(lows + grads, axis=0)
        hat[...] = mm(jnp.concatenate([both, both], axis=1), fwd_ref[...])

        conv_in, back_in = [], []
        for k in range(ng):
            r = slice(GROUP * k, GROUP * (k + 1))
            rg = slice(SUB + GROUP * k, SUB + GROUP * (k + 1))
            ca, cb, cc = (row(red, i, slice(k, k + 1)) for i in range(3))
            pr, pi = hat[r, :LANES], hat[r, LANES:]
            gr, gi = hat[rg, :LANES], hat[rg, LANES:]
            conv_in.append(
                jnp.concatenate([pr * ca - pi * cb, pr * cb + pi * cc], axis=1).astype(BF16)
            )
            back_in.append(
                jnp.concatenate([gr * ca + gi * cb, gi * cc - gr * cb], axis=1).astype(BF16)
            )
            for i, value in enumerate((pr * gr, pi * gi, pr * gi - pi * gr)):
                red[3 + i, 8 * k : 8 * k + 8, :] = value[:8] + value[8:]
        spec = jnp.concatenate(conv_in + back_in, axis=0)
        res[...] = mm(jnp.concatenate([spec, spec], axis=1), inv_ref[...])

        sums = []
        for k in range(ng):
            r = slice(GROUP * k, GROUP * (k + 1))
            rg = slice(SUB + GROUP * k, SUB + GROUP * (k + 1))
            cot = cot_ref[pl.ds(base + GROUP * k, GROUP), :].astype(F32)
            kf, vf, product, gm = (feat[i, r] for i in range(4))
            sk = skip_cols[r]
            gq = cot * (res[r] + sk * product)
            gp = res[rg] + sk * gm
            gf = [gq, gp * vf, gp * kf]
            sums.append((gm * product).astype(BF16))
            gfb = jnp.concatenate([g.astype(BF16) for g in gf], axis=0)
            xsb = jnp.concatenate(
                [xs[r, LANES * j : LANES * (j + 1)].astype(BF16) for j in range(taps)]
                + [jnp.zeros((GROUP, LANES), BF16)] * (LANES // GROUP - taps),
                axis=0,
            )
            corr = nt(gfb, xsb)
            for m in range(3):
                kept = jnp.where(own, corr[GROUP * m : GROUP * (m + 1)], 0.0)
                red[6 + m, 8 * k : 8 * k + 8, :] = kept[:8] + kept[8:]
            if not last:
                parts = []
                for j in range(taps):
                    total = None
                    for m in range(3):
                        term = row(fsp, m * taps + j, slice(k, k + 1)) * gf[m]
                        total = term if total is None else total + term
                    parts.append(total.astype(BF16))
                hats = jnp.concatenate(parts, axis=1)
                gin = cot + mm(hats, unshift_ref[...])
                gin_ref[pl.ds(base + GROUP * k, GROUP), :] = gin.astype(BF16)
        for i in range(6):
            total = red[3 + i, pl.ds(0, ng, stride=8), :]
            for s in range(1, 8):
                total = total + red[3 + i, pl.ds(s, ng, stride=8), :]
            acc[i, pl.ds(gbase, ng), :] = total
        ones = jnp.ones((8, LANES), BF16)
        skips[pl.ds(index, 1), :] = nt(ones, jnp.concatenate(sums, axis=0))[:1]
        return 0

    lax.fori_loop(0, channels // SUB, block, 0)

    if last:
        total = [acc[i] + acc_in[i] for i in range(6)]
        real = total[0] + jnp.where(first, 0.0, total[1])
        imag = jnp.where(first, total[1], total[2])
        msg_ref[:groups] = mm(jnp.concatenate([real, imag], axis=1), finv_ref[...], PRECISE)
        at = groups
        count = channels // LANES
        msg_ref[at : at + count] = skips[...] + skip_in[...]
        at += count
        pick = (
            lax.broadcasted_iota(jnp.int32, (8, LANES), 1) // GROUP
            == lax.broadcasted_iota(jnp.int32, (8, LANES), 0)
        ).astype(F32)
        for m in range(3):
            for q in range(groups // LANES):
                part = total[3 + m][LANES * q : LANES * (q + 1)]
                msg_ref[at : at + 8] = nt(pick, part, PRECISE)
                at += 8


def run_tick(saved, cot, filters, medium, skip_rows, tick, prior):
    last = prior is not None
    channels, length = saved.shape[-2:]
    groups = filters.shape[2]
    taps = filters.shape[3]
    forward, inverse, inverse_full, shift, unshift = tables(length, taps)
    ng = SUB // GROUP
    full = lambda a: pl.BlockSpec(a.shape, lambda i: (0,) * a.ndim)
    x_spec = pl.BlockSpec((1, 1, 1, channels, length), lambda i: (0, tick, 0, 0, 0))
    ins = [saved, cot, filters, medium, skip_rows, forward, inverse, shift]
    ins += [inverse_full, *prior] if last else [unshift]
    acc_shape = (6, groups, LANES)
    skip_shape = (channels // LANES, LANES)
    scratch = [
        pltpu.VMEM((3 * taps, ng, LANES), F32),
        pltpu.VMEM((3, groups, LANES), F32),
        pltpu.VMEM((SUB, taps * LANES), F32),
        pltpu.VMEM((4, SUB, LANES), F32),
        pltpu.VMEM((2 * SUB, 2 * LANES), F32),
        pltpu.VMEM((2 * SUB, LANES), F32),
        pltpu.VMEM((9, 8 * ng, LANES), F32),
    ]
    if last:
        outs = [jax.ShapeDtypeStruct((groups + channels // LANES + 24 * (groups // LANES), LANES), F32)]
        scratch += [pltpu.VMEM(acc_shape, F32), pltpu.VMEM(skip_shape, F32)]
    else:
        outs = [
            jax.ShapeDtypeStruct((channels, length), BF16),
            jax.ShapeDtypeStruct(acc_shape, F32),
            jax.ShapeDtypeStruct(skip_shape, F32),
        ]
    return pl.pallas_call(
        functools.partial(tick_kernel, last, taps),
        out_shape=outs,
        grid=(1,),
        in_specs=[x_spec] + [full(a) for a in ins[1:]],
        out_specs=[full(a) for a in outs],
        scratch_shapes=scratch,
        compiler_params=pltpu.CompilerParams(vmem_limit_bytes=48 << 20),
        name="last_tick" if last else "first_tick",
    )(*ins)


def finish_kernel(count, taps, *refs):
    ins, (short_ref, medium_ref, skip_ref) = refs[:count], refs[count:]
    total = ins[0][...]
    for ref in ins[1:]:
        total = total + ref[...]
    total = total * (1.0 / count)
    groups = medium_ref.shape[1]
    channels = skip_ref.shape[1]
    medium_ref[0] = total[:groups]
    at = groups
    for i in range(channels // LANES):
        skip_ref[:, LANES * i : LANES * (i + 1)] = total[at : at + 1]
        at += 1
    for m in range(3):
        for q in range(groups // LANES):
            short_ref[0, m, LANES * q : LANES * (q + 1), :] = total[at : at + 8].T[:, :taps]
            at += 8


def finish(parts, groups, channels, taps):
    return pl.pallas_call(
        functools.partial(finish_kernel, len(parts), taps),
        out_shape=(
            jax.ShapeDtypeStruct((1, 3, groups, taps), F32),
            jax.ShapeDtypeStruct((1, groups, LANES), F32),
            jax.ShapeDtypeStruct((1, channels), F32),
        ),
        name="finish",
    )(*parts)


def body(saved, upstream, short_filters, medium_filter, skip):
    channels, length = saved.shape[-2:]
    ticks = saved.shape[1]
    groups, taps = short_filters.shape[2:]
    replicas = lax.axis_size("replica")
    skip_rows = skip.reshape(channels // LANES, LANES)
    incoming = upstream[0, 0]
    gin, acc, skips = run_tick(saved, incoming, short_filters, medium_filter, skip_rows, 0, None)
    incoming = shifted(gin, "section", -1)
    (message,) = run_tick(
        saved, incoming, short_filters, medium_filter, skip_rows, 1, (acc, skips)
    )
    parts = [message] + [
        lax.ppermute(message, "replica", [(i, (i + by) % replicas) for i in range(replicas)])
        for by in range(1, replicas)
    ]
    return finish(parts, groups, channels, taps)


def solution(mesh):
    placed = (
        P("section", None, "replica", None, None),
        P("section", "replica", None, None),
        P("section", None, None, None),
        P("section", None, None),
        P("section", None),
    )
    return jax.shard_map(
        body,
        mesh=mesh,
        in_specs=placed,
        out_specs=(P("section", None, None, None), P("section", None, None), P("section", None)),
        check_vma=False,
    )
```

profile of v0, /device:TPU:4, one launch (start us, length us, event | category | flops | bytes accessed | tf_op | source)
XLA Modules:
  0.0 108.6 jit_solution(7954327851393161653)
XLA Ops:
  0.6 0.9 copy.13.refs_2_
  1.5 0.0 copy-start
  1.6 1.6 %copy-done = bf16[1,2,1,4096,128]{4,3,2,1,0:T(8,128)(2,1)S(1)} copy-done((bf16[1,2,1,4096,128]{4,3,2,1,0:T(8,128)(2,1)S(1)}, bf16[1,2,1,4096,128]{4,3,2,1,0:T(8,128)(2,1)}, u32[]{:S(2)}) %copy-start) | copy-done | bytes 2097176
  3.1 0.0 copy-start.1
  3.1 1.2 %copy-done.1 = bf16[1,1,4096,128]{3,2,1,0:T(8,128)(2,1)S(1)} copy-done((bf16[1,1,4096,128]{3,2,1,0:T(8,128)(2,1)S(1)}, bf16[1,1,4096,128]{3,2,1,0:T(8,128)(2,1)}, u32[]{:S(2)}) %copy-start.1) | copy-done | bytes 1048600
  4.4 0.0 copy-start.2
  4.4 0.9 copy-done.2
  5.3 0.0 copy-start.4
  5.3 0.9 copy-done.4
  6.2 0.0 copy-start.5
  6.2 0.9 copy-done.5
  7.1 0.0 copy-start.7
  7.1 0.9 copy-done.7
  8.0 0.0 copy-start.8
  8.0 0.9 copy-done.8
  8.9 0.0 copy-start.10
  8.9 0.7 copy-done.10
  9.7 0.0 copy-start.6
  9.7 0.0 copy-start.9
  9.7 0.0 copy-start.11
  9.7 33.7 %first_tick.1 = (bf16[4096,128]{1,0:T(8,128)(2,1)S(1)}, f32[6,256,128]{2,1,0:T(8,128)S(1)}, f32[32,128]{1,0:T(8,128)S(1)}) custom-call(bf16[1,2,1,4096,128]{4,3,2,1,0:T(8,128)(2,1)S(1)} %copy-done, bf16[4096,128]{1,0:T(8,128)(2,1)S(1)} %bitcast.2, f32[1,3,256,7]{3,2,1,0:T(8,128)S(1)} %copy.13.refs_2_, f32[1,256,128]{2,1,0:T(8,128)S(1)} %copy-done.4, ...), custom_call_target="tpu_custom_call" | custom-call | tf_op jit(solution)/shard_map/first_tick/pallas_call | solution.py:242
  43.4 2.8 %collective-permute-start = (bf16[4096,128]{1,0:T(8,128)(2,1)S(1)}, bf16[4096,128]{1,0:T(8,128)(2,1)S(1)}, u32[]{:S(2)}, u32[]{:S(2)}) collective-permute-start(bf16[4096,128]{1,0:T(8,128)(2,1)S(1)} %get-tuple-element.6), channel_id=1, source_target_pairs={{4,0},{8,4},{12,8},{16,12},{20,16},{24,20},{28,24},{5,1},{9,5},{13... | collective-permute-start | bytes 3145736 | tf_op jit(solution)/shard_map/ppermute | solution.py:23
  46.2 12.3 %collective-permute-done.refs_1_ = bf16[4096,128]{1,0:T(8,128)(2,1)S(1)} collective-permute-done((bf16[4096,128]{1,0:T(8,128)(2,1)S(1)}, bf16[4096,128]{1,0:T(8,128)(2,1)S(1)}, u32[]{:S(2)}, u32[]{:S(2)}) %collective-permute-start) | collective-permute-done | bytes 1048608 | tf_op jit(solution)/shard_map/ppermute | solution.py:23
  58.5 0.0 copy-done.6
  58.5 0.0 copy-done.9
  58.5 0.0 copy-done.11
  58.5 25.6 %last_tick.1.refs_0_ = f32[336,128]{1,0:T(8,128)S(1)} custom-call(bf16[1,2,1,4096,128]{4,3,2,1,0:T(8,128)(2,1)S(1)} %copy-done, bf16[4096,128]{1,0:T(8,128)(2,1)S(1)} %collective-permute-done.refs_1_, f32[1,3,256,7]{3,2,1,0:T(8,128)S(1)} %copy.13.refs_2_, f32[1,256,128]{2,1,0:T(8,128)S(1)} %copy-done.4, f32[32,128]{1,0:T(8,128)S(1)} %bitcast.4, ...), custom_call_target="tpu_custom_call" | custom-call | tf_op jit(solution)/shard_map/last_tick/pallas_call | solution.py:242
  84.1 0.0 copy-start.3
  84.1 3.6 %collective-permute-start.3 = (f32[336,128]{1,0:T(8,128)S(1)}, f32[336,128]{1,0:T(8,128)S(1)}, u32[]{:S(2)}, u32[]{:S(2)}) collective-permute-start(f32[336,128]{1,0:T(8,128)S(1)} %last_tick.1.refs_0_), channel_id=1, source_target_pairs={{0,3},{1,0},{2,1},{3,2},{4,7},{5,4},{6,5},{7,6},{8,11},{9,8},{10,9... | collective-permute-start | bytes 516104 | tf_op jit(solution)/shard_map/ppermute | solution.py:298
  87.7 0.0 collective-permute-start.2
  87.7 1.0 collective-permute-start.1
  88.7 3.8 %collective-permute-done.3.refs_3_ = f32[336,128]{1,0:T(8,128)S(1)} collective-permute-done((f32[336,128]{1,0:T(8,128)S(1)}, f32[336,128]{1,0:T(8,128)S(1)}, u32[]{:S(2)}, u32[]{:S(2)}) %collective-permute-start.3) | collective-permute-done | bytes 172064 | tf_op jit(solution)/shard_map/ppermute | solution.py:298
  92.6 0.0 copy-start.12
  92.6 10.8 %collective-permute-done.2.refs_2_ = f32[336,128]{1,0:T(8,128)S(1)} collective-permute-done((f32[336,128]{1,0:T(8,128)S(1)}, f32[336,128]{1,0:T(8,128)S(1)}, u32[]{:S(2)}, u32[]{:S(2)}) %collective-permute-start.2) | collective-permute-done | bytes 172064 | tf_op jit(solution)/shard_map/ppermute | solution.py:298
  103.4 0.0 copy-start.13
  103.4 0.0 collective-permute-done.1.refs_1_
  103.4 0.0 copy-done.3
  103.4 0.0 copy-done.12
  103.4 0.6 copy-done.13
  104.0 0.0 copy-start.14
  104.0 0.7 copy-done.14
  104.7 2.1 %finish.1 = (f32[1,3,256,7]{3,2,1,0:T(8,128)}, f32[1,256,128]{2,1,0:T(8,128)}, f32[1,4096]{1,0:T(1,128)}) custom-call(f32[336,128]{1,0:T(8,128)} %copy-done.3, f32[336,128]{1,0:T(8,128)} %copy-done.14, f32[336,128]{1,0:T(8,128)} %copy-done.13, f32[336,128]{1,0:T(8,128)} %copy-done.12), custom_call_target="tpu_custom_call" | custom-call | tf_op jit(solution)/shard_map/finish/pallas_call | solution.py:274
  106.8 1.8 %copy.15 = f32[1,3,256,7]{2,0,3,1:T(1,128)} copy(f32[1,3,256,7]{3,2,1,0:T(8,128)} %get-tuple-element.9) | data formatting | bytes 43008 | tf_op jit(solution)/shard_map/finish/pallas_call | solution.py:274
Async XLA Ops:
  1.5 1.6 %copy-start = (bf16[1,2,1,4096,128]{4,3,2,1,0:T(8,128)(2,1)S(1)}, bf16[1,2,1,4096,128]{4,3,2,1,0:T(8,128)(2,1)}, u32[]{:S(2)}) copy-start(bf16[1,2,1,4096,128]{4,3,2,1,0:T(8,128)(2,1)} %refs_0_.3) | copy-start | bytes 6291460
  3.1 1.2 %copy-start.1 = (bf16[1,1,4096,128]{3,2,1,0:T(8,128)(2,1)S(1)}, bf16[1,1,4096,128]{3,2,1,0:T(8,128)(2,1)}, u32[]{:S(2)}) copy-start(bf16[1,1,4096,128]{3,2,1,0:T(8,128)(2,1)} %param.11) | copy-start | bytes 3145732
  4.4 0.9 copy-start.2
  5.3 0.9 copy-start.4
  6.2 0.9 copy-start.5
  7.1 0.9 copy-start.7
  8.0 0.9 copy-start.8
  8.9 0.7 copy-start.10
  9.7 48.8 %copy-start.6 = (bf16[512,128]{1,0:T(8,128)(2,1)S(1)}, bf16[512,128]{1,0:T(8,128)(2,1)}, u32[]{:S(2)}) copy-start(bf16[512,128]{1,0:T(8,128)(2,1)} %constant.11.clone.refs_6_) | copy-start | bytes 393220
  9.7 48.8 %copy-start.9 = (f32[256,128]{1,0:T(8,128)S(1)}, f32[256,128]{1,0:T(8,128)}, u32[]{:S(2)}) copy-start(f32[256,128]{1,0:T(8,128)} %constant.14.clone.refs_8_) | copy-start | bytes 393220
  9.7 48.8 %copy-start.11 = (f32[1,4096]{1,0:T(1,128)S(1)}, f32[1,4096]{1,0:T(1,128)}, u32[]{:S(2)}) copy-start(f32[1,4096]{1,0:T(1,128)} %param.14) | copy-start | bytes 49156
  43.4 15.1 %collective-permute-start = (bf16[4096,128]{1,0:T(8,128)(2,1)S(1)}, bf16[4096,128]{1,0:T(8,128)(2,1)S(1)}, u32[]{:S(2)}, u32[]{:S(2)}) collective-permute-start(bf16[4096,128]{1,0:T(8,128)(2,1)S(1)} %get-tuple-element.6), channel_id=1, source_target_pairs={{4,0},{8,4},{12,8},{16,12},{20,16},{24,20},{28,24},{5,1},{9,5},{13... | collective-permute-start | bytes 3145736 | tf_op jit(solution)/shard_map/ppermute | solution.py:23
  84.1 19.3 %copy-start.3 = (f32[336,128]{1,0:T(8,128)}, f32[336,128]{1,0:T(8,128)S(1)}, u32[]{:S(2)}) copy-start(f32[336,128]{1,0:T(8,128)S(1)} %last_tick.1.refs_0_) | copy-start | bytes 516100
  84.1 8.5 %collective-permute-start.3 = (f32[336,128]{1,0:T(8,128)S(1)}, f32[336,128]{1,0:T(8,128)S(1)}, u32[]{:S(2)}, u32[]{:S(2)}) collective-permute-start(f32[336,128]{1,0:T(8,128)S(1)} %last_tick.1.refs_0_), channel_id=1, source_target_pairs={{0,3},{1,0},{2,1},{3,2},{4,7},{5,4},{6,5},{7,6},{8,11},{9,8},{10,9... | collective-permute-start | bytes 516104 | tf_op jit(solution)/shard_map/ppermute | solution.py:298
  87.7 15.7 %collective-permute-start.2 = (f32[336,128]{1,0:T(8,128)S(1)}, f32[336,128]{1,0:T(8,128)S(1)}, u32[]{:S(2)}, u32[]{:S(2)}) collective-permute-start(f32[336,128]{1,0:T(8,128)S(1)} %last_tick.1.refs_0_), channel_id=1, source_target_pairs={{0,2},{1,3},{2,0},{3,1},{4,6},{5,7},{6,4},{7,5},{8,10},{9,11},{10,... | collective-permute-start | bytes 516104 | tf_op jit(solution)/shard_map/ppermute | solution.py:298
  87.7 15.7 %collective-permute-start.1 = (f32[336,128]{1,0:T(8,128)S(1)}, f32[336,128]{1,0:T(8,128)S(1)}, u32[]{:S(2)}, u32[]{:S(2)}) collective-permute-start(f32[336,128]{1,0:T(8,128)S(1)} %last_tick.1.refs_0_), channel_id=1, source_target_pairs={{0,1},{1,2},{2,3},{3,0},{4,5},{5,6},{6,7},{7,4},{8,9},{9,10},{10,1... | collective-permute-start | bytes 516104 | tf_op jit(solution)/shard_map/ppermute | solution.py:298
  92.6 10.8 %copy-start.12 = (f32[336,128]{1,0:T(8,128)}, f32[336,128]{1,0:T(8,128)S(1)}, u32[]{:S(2)}) copy-start(f32[336,128]{1,0:T(8,128)S(1)} %collective-permute-done.3.refs_3_) | copy-start | bytes 516100
  103.4 0.7 copy-start.13
  104.0 0.7 copy-start.14
where the time goes:
time: 109 us
  Pallas kernels  61.4 us (56%)
  waiting for transfers between devices  26.9 us (25%)
  local copies, waits for them, and re-layouts  12.1 us (11%)
  starting transfers between devices  7.41 us (7%)
    pallas_call x2, Pallas kernels, run_tick(): pl.pallas_call(functools.partial(tick_kernel, last, taps), out_shape=outs...  59.3 us
    ppermute x3, waiting for transfers between devices, body(): lax.ppermute(message, 'replica', [(i, (i + by) % replicas) for i in range...  14.6 us
    ppermute x1, waiting for transfers between devices, shifted(): return lax.ppermute(array, axis, pairs)  12.3 us
    unnamed x31, local copies, waits for them, and re-layouts  10.3 us
    ppermute x3, starting transfers between devices, body(): lax.ppermute(message, 'replica', [(i, (i + by) % replicas) for i in range...  4.63 us
    ppermute x1, starting transfers between devices, shifted(): return lax.ppermute(array, axis, pairs)  2.78 us
  transfers between devices with their start and end apart: 4, of which 3 were waited for; matrix products, arithmetic and copies ran while one was open for 0% of the time, Pallas kernels for 0%

commit v1 on v0

v1 whole, which is shorter than its diff:
```python
import functools

import jax
import jax.numpy as jnp
import numpy as np
from jax import lax
from jax.experimental import pallas as pl
from jax.experimental.pallas import tpu as pltpu
from jax.sharding import PartitionSpec as P

GROUP = 16
LANES = 128
SUB = 128

F32 = jnp.float32
BF16 = jnp.bfloat16
PRECISE = lax.Precision.HIGHEST


def shifted(array, axis, by):
    count = lax.axis_size(axis)
    pairs = [(i, i + by) for i in range(count) if 0 <= i + by < count]
    return lax.ppermute(array, axis, pairs)


def split(matrix):
    high = matrix.astype(jnp.bfloat16)
    low = (matrix - high.astype(np.float64)).astype(jnp.bfloat16)
    return high, low


@functools.lru_cache(None)
def tables(length, taps):
    points = 2 * length
    pos = np.arange(length)[:, None]
    freq = np.arange(length)[None, :]
    angle = 2.0 * np.pi * ((pos * freq) % points) / points
    real, imag = np.cos(angle), -np.sin(angle)
    imag[:, 0] = 1.0 - 2.0 * (np.arange(length) % 2)
    forward = np.concatenate([real, imag], axis=1)
    weight = np.full((2 * length, 1), 2.0 / points)
    weight[0] = weight[length] = 1.0 / points
    inverse = weight * forward.T
    shift = np.concatenate([np.eye(length, k=lag) for lag in range(1, taps)], axis=1)
    unshift = np.concatenate([np.eye(length, k=-lag) for lag in range(taps)], axis=0)
    return (
        np.concatenate(split(forward), axis=0),
        np.concatenate(split(inverse), axis=0),
        inverse.astype(np.float32),
        shift.astype(jnp.bfloat16),
        unshift.astype(jnp.bfloat16),
    )


def nt(left, right, precision=None):
    return lax.dot_general(
        left, right, (((1,), (1,)), ((), ())), precision=precision, preferred_element_type=F32
    )


def mm(left, right, precision=None):
    return jnp.dot(left, right, precision=precision, preferred_element_type=F32)


def row(ref, *index):
    return jnp.broadcast_to(ref[index], (GROUP, LANES))


def own_channel():
    lane = lax.broadcasted_iota(jnp.int32, (GROUP, LANES), 1)
    return lax.rem(lane, GROUP) == lax.broadcasted_iota(jnp.int32, (GROUP, LANES), 0)


class Tick:
    def __init__(self, last, taps, ins, outs, scratch):
        self.last, self.taps, self.ng = last, taps, SUB // GROUP
        (self.x, self.cot, self.f, self.med, self.skip, self.fwd, self.inv, self.shift) = ins[:8]
        if last:
            (self.finv, self.acc_in, self.skip_in) = ins[8:]
            (self.msg,) = outs
            self.acc, self.skips = scratch[-2:]
        else:
            (self.unshift,) = ins[8:]
            self.gin, self.acc, self.skips = outs
        self.columns, self.coef = scratch[:2]
        self.slots = (scratch[2:9], scratch[9:16])
        self.spec, self.res, self.red, self.sums, self.hats, self.turn = scratch[16:22]

    def rows(self, block):
        return pl.multiple_of(block * SUB, SUB)

    def groups(self, block):
        return pl.ds(pl.multiple_of(block * self.ng, self.ng), self.ng)

    def setup(self):
        first = lax.broadcasted_iota(jnp.int32, (1, LANES), 1) == 0
        h = self.med[0].astype(BF16)
        hh = mm(jnp.concatenate([h, h], axis=1), self.fwd[...])
        hr, hi = hh[:, :LANES], hh[:, LANES:]
        self.coef[0] = hr
        self.coef[1] = jnp.where(first, 0.0, hi)
        self.coef[2] = jnp.where(first, hi, hr)
        self.turn[...] = jnp.zeros_like(self.turn)
        for q in range(h.shape[0] // LANES):
            cols = slice(LANES * q, LANES * (q + 1))
            for m in range(3):
                for j in range(self.taps):
                    t = m * self.taps + j
                    self.turn[t : t + 1, :] = self.f[m, j, :, cols]
            self.columns[cols, :] = self.turn[...].T

    def start(self, block, slot):
        taps_at, coef_at, skip_at, xs, _, _, _ = self.slots[slot]
        x = self.x[0, 0, 0, pl.ds(self.rows(block), SUB), :]
        xs[:, LANES:] = mm(x, self.shift[...])
        xs[:, :LANES] = x.astype(F32)
        mine = self.columns[self.groups(block), :]
        for t in range(3 * self.taps):
            taps_at[t] = jnp.broadcast_to(mine[:, t : t + 1], (self.ng, LANES))
        for i in range(3):
            coef_at[i] = self.coef[i, self.groups(block), :]
        skip_at[...] = jnp.broadcast_to(self.skip[pl.ds(block, 1), :], (SUB, LANES)).T

    def features(self, block, slot):
        taps_at, _, _, xs, feat, lows, _ = self.slots[slot]
        for k in range(self.ng):
            r = slice(GROUP * k, GROUP * (k + 1))
            rg = slice(SUB + GROUP * k, SUB + GROUP * (k + 1))
            f = []
            for m in range(3):
                total = None
                for j in range(self.taps):
                    tap = row(taps_at, m * self.taps + j, slice(k, k + 1))
                    term = tap * xs[r, LANES * j : LANES * (j + 1)]
                    total = term if total is None else total + term
                f.append(total)
            product = f[1] * f[2]
            gm = self.cot[pl.ds(self.rows(block) + GROUP * k, GROUP), :].astype(F32) * f[0]
            feat[0, r] = f[1]
            feat[1, r] = f[2]
            feat[2, r] = product
            feat[3, r] = gm
            lows[r] = product.astype(BF16)
            lows[rg] = gm.astype(BF16)

    def spectra(self, slot):
        lows, hat = self.slots[slot][5:]
        low = lows[...]
        hat[...] = mm(jnp.concatenate([low, low], axis=1), self.fwd[...])

    def filter(self, slot):
        _, coef_at, _, _, _, _, hat = self.slots[slot]
        spec, red = self.spec, self.red
        for k in range(self.ng):
            r = slice(GROUP * k, GROUP * (k + 1))
            rg = slice(SUB + GROUP * k, SUB + GROUP * (k + 1))
            ca, cb, cc = (row(coef_at, i, slice(k, k + 1)) for i in range(3))
            pr, pi = hat[r, :LANES], hat[r, LANES:]
            gr, gi = hat[rg, :LANES], hat[rg, LANES:]
            spec[r, :LANES] = (pr * ca - pi * cb).astype(BF16)
            spec[r, LANES:] = (pr * cb + pi * cc).astype(BF16)
            spec[rg, :LANES] = (gr * ca + gi * cb).astype(BF16)
            spec[rg, LANES:] = (gi * cc - gr * cb).astype(BF16)
            for i, value in enumerate((pr * gr, pi * gi, pr * gi - pi * gr)):
                red[i, 8 * k : 8 * k + 8, :] = value[:8] + value[8:]

    def invert(self):
        both = self.spec[...]
        self.res[...] = mm(jnp.concatenate([both, both], axis=1), self.inv[...])

    def gradients(self, block, slot):
        taps_at, _, skip_at, xs, feat, _, _ = self.slots[slot]
        own = own_channel()
        for k in range(self.ng):
            r = slice(GROUP * k, GROUP * (k + 1))
            rg = slice(SUB + GROUP * k, SUB + GROUP * (k + 1))
            cot = self.cot[pl.ds(self.rows(block) + GROUP * k, GROUP), :].astype(F32)
            kf, vf, product, gm = (feat[i, r] for i in range(4))
            sk = skip_at[r]
            gq = cot * (self.res[r] + sk * product)
            gp = self.res[rg] + sk * gm
            gf = [gq, gp * vf, gp * kf]
            self.sums[r] = (gm * product).astype(BF16)
            gfb = jnp.concatenate([g.astype(BF16) for g in gf], axis=0)
            xsb = jnp.concatenate(
                [xs[r, LANES * j : LANES * (j + 1)].astype(BF16) for j in range(self.taps)]
                + [jnp.zeros((GROUP, LANES), BF16)] * (LANES // GROUP - self.taps),
                axis=0,
            )
            corr = nt(gfb, xsb)
            if not self.last:
                for j in range(self.taps):
                    total = None
                    for m in range(3):
                        tap = row(taps_at, m * self.taps + j, slice(k, k + 1))
                        total = tap * gf[m] if total is None else total + tap * gf[m]
                    self.hats[r, LANES * j : LANES * (j + 1)] = total.astype(BF16)
            for m in range(3):
                kept = jnp.where(own, corr[GROUP * m : GROUP * (m + 1)], 0.0)
                self.red[3 + m, 8 * k : 8 * k + 8, :] = kept[:8] + kept[8:]

    def reduce(self, block, terms):
        for i in terms:
            total = self.red[i, pl.ds(0, self.ng, stride=8), :]
            for s in range(1, 8):
                total = total + self.red[i, pl.ds(s, self.ng, stride=8), :]
            self.acc[i, self.groups(block), :] = total

    def finish(self, block):
        if not self.last:
            rows = pl.ds(self.rows(block), SUB)
            gin = mm(self.hats[...], self.unshift[...]) + self.cot[rows, :].astype(F32)
            self.gin[rows, :] = gin.astype(BF16)
        self.skips[pl.ds(block, 1), :] = nt(jnp.ones((8, LANES), BF16), self.sums[...])[:1]
        self.reduce(block, range(3, 6))

    def step(self, block, blocks, slot):
        after = jnp.minimum(block + 1, blocks - 1)
        self.start(after, 1 - slot)
        self.filter(slot)
        self.invert()
        self.finish(jnp.maximum(block - 1, 0))
        self.features(after, 1 - slot)
        self.reduce(block, range(3))
        self.spectra(1 - slot)
        self.gradients(block, slot)

    def message(self):
        first = lax.broadcasted_iota(jnp.int32, (1, LANES), 1) == 0
        total = [self.acc[i] + self.acc_in[i] for i in range(6)]
        real = total[0] + jnp.where(first, 0.0, total[1])
        imag = jnp.where(first, total[1], total[2])
        at = real.shape[0]
        both = jnp.concatenate([real, imag], axis=1)
        self.msg[:at] = mm(both, self.finv[...], PRECISE)
        count = self.skips.shape[0]
        self.msg[at : at + count] = self.skips[...] + self.skip_in[...]
        at += count
        pick = (
            lax.broadcasted_iota(jnp.int32, (8, LANES), 1) // GROUP
            == lax.broadcasted_iota(jnp.int32, (8, LANES), 0)
        ).astype(F32)
        for m in range(3):
            for q in range(real.shape[0] // LANES):
                part = total[3 + m][LANES * q : LANES * (q + 1)]
                self.msg[at : at + 8] = nt(pick, part, PRECISE)
                at += 8


def tick_kernel(last, taps, counts, *refs):
    ins, outs, scratch = refs[: counts[0]], refs[counts[0] : sum(counts)], refs[sum(counts) :]
    tick = Tick(last, taps, ins, outs, scratch)
    blocks = tick.x.shape[-2] // SUB
    tick.setup()
    tick.start(0, 0)
    tick.features(0, 0)
    tick.spectra(0)

    def pair(index, _):
        tick.step(2 * index, blocks, 0)
        tick.step(2 * index + 1, blocks, 1)
        return 0

    lax.fori_loop(0, blocks // 2, pair, 0)
    tick.finish(blocks - 1)
    if last:
        tick.message()


def in_hbm(array):
    return pltpu.with_memory_space_constraint(array, pltpu.HBM)


def run_tick(saved, cot, filters, medium, skip_rows, tick, prior):
    last = prior is not None
    channels, length = saved.shape[-2:]
    taps = filters.shape[1]
    groups = filters.shape[3]
    forward, inverse, inverse_full, shift, unshift = tables(length, taps)
    ng = SUB // GROUP
    full = lambda a: pl.BlockSpec(a.shape, lambda i: (0,) * a.ndim)
    x_spec = pl.BlockSpec((1, 1, 1, channels, length), lambda i: (0, tick, 0, 0, 0))
    ins = [saved, cot, filters, medium, skip_rows, forward, inverse, shift]
    ins += [inverse_full] if last else [unshift]
    ins = [in_hbm(jnp.asarray(a)) for a in ins]
    ins += [*prior] if last else []
    acc_shape = (6, groups, LANES)
    skip_shape = (channels // LANES, LANES)
    slot = [
        pltpu.VMEM((3 * taps, ng, LANES), F32),
        pltpu.VMEM((3, ng, LANES), F32),
        pltpu.VMEM((SUB, LANES), F32),
        pltpu.VMEM((SUB, taps * LANES), F32),
        pltpu.VMEM((4, SUB, LANES), F32),
        pltpu.VMEM((2 * SUB, LANES), BF16),
        pltpu.VMEM((2 * SUB, 2 * LANES), F32),
    ]
    scratch = [pltpu.VMEM((groups, LANES), F32), pltpu.VMEM((3, groups, LANES), F32)]
    scratch += slot + slot
    scratch += [
        pltpu.VMEM((2 * SUB, 2 * LANES), BF16),
        pltpu.VMEM((2 * SUB, LANES), F32),
        pltpu.VMEM((6, 8 * ng, LANES), F32),
        pltpu.VMEM((SUB, LANES), BF16),
        pltpu.VMEM((SUB, taps * LANES), BF16),
        pltpu.VMEM((LANES, LANES), F32),
    ]
    if last:
        outs = [jax.ShapeDtypeStruct((groups + channels // LANES + 24 * (groups // LANES), LANES), F32)]
        scratch += [pltpu.VMEM(acc_shape, F32), pltpu.VMEM(skip_shape, F32)]
    else:
        outs = [
            jax.ShapeDtypeStruct((channels, length), BF16),
            jax.ShapeDtypeStruct(acc_shape, F32),
            jax.ShapeDtypeStruct(skip_shape, F32),
        ]
    return pl.pallas_call(
        functools.partial(tick_kernel, last, taps, (len(ins), len(outs))),
        out_shape=outs,
        grid=(1,),
        in_specs=[x_spec] + [full(a) for a in ins[1:]],
        out_specs=[full(a) for a in outs],
        scratch_shapes=scratch,
        compiler_params=pltpu.CompilerParams(vmem_limit_bytes=48 << 20),
        name="last_tick" if last else "first_tick",
    )(*ins)


def finish_kernel(count, taps, *refs):
    ins, (short_ref, medium_ref, skip_ref) = refs[:count], refs[count:]
    total = ins[0][...]
    for ref in ins[1:]:
        total = total + ref[...]
    total = total * (1.0 / count)
    groups = medium_ref.shape[0]
    medium_ref[...] = total[:groups]
    at = groups + skip_ref.shape[0]
    skip_ref[...] = total[groups:at]
    for m in range(3):
        for q in range(groups // LANES):
            for j in range(taps):
                short_ref[m, j, :, LANES * q : LANES * (q + 1)] = total[at + j : at + j + 1]
            at += 8


def finish(parts, groups, channels, taps):
    vmem = pl.BlockSpec(memory_space=pltpu.VMEM)
    return pl.pallas_call(
        functools.partial(finish_kernel, len(parts), taps),
        out_shape=(
            jax.ShapeDtypeStruct((3, taps, 1, groups), F32),
            jax.ShapeDtypeStruct((groups, LANES), F32),
            jax.ShapeDtypeStruct((channels // LANES, LANES), F32),
        ),
        in_specs=[vmem] * len(parts),
        out_specs=[vmem] * 3,
        name="finish",
    )(*parts)


def body(saved, upstream, short_filters, medium_filter, skip):
    channels, length = saved.shape[-2:]
    groups, taps = short_filters.shape[2:]
    replicas = lax.axis_size("replica")
    skip_rows = skip.reshape(channels // LANES, LANES)
    filters = jnp.transpose(short_filters, (1, 3, 0, 2))
    incoming = upstream[0, 0]
    gin, acc, skips = run_tick(saved, incoming, filters, medium_filter, skip_rows, 0, None)
    incoming = shifted(gin, "section", -1)
    (message,) = run_tick(saved, incoming, filters, medium_filter, skip_rows, 1, (acc, skips))
    parts = [message] + [
        lax.ppermute(message, "replica", [(i, (i + by) % replicas) for i in range(replicas)])
        for by in range(1, replicas)
    ]
    short, medium, skip_grad = finish(parts, groups, channels, taps)
    return (
        jnp.transpose(short, (2, 0, 3, 1)),
        medium[None],
        skip_grad.reshape(1, channels),
    )


def solution(mesh):
    placed = (
        P("section", None, "replica", None, None),
        P("section", "replica", None, None),
        P("section", None, None, None),
        P("section", None, None),
        P("section", None),
    )
    return jax.shard_map(
        body,
        mesh=mesh,
        in_specs=placed,
        out_specs=(P("section", None, None, None), P("section", None, None), P("section", None)),
        check_vma=False,
    )
```

time: 109 us -> 80.7 us (0.74)
  Pallas kernels: 61.4 us -> 43 us
  local copies, waits for them, and re-layouts: 12.1 us -> 2.3 us
    pallas_call x2, Pallas kernels: 59.3 us -> 41.2 us  [run_tick(): pl.pallas_call(functools.partial(tick_kernel, last, taps, (len(ins), len(...]
    unnamed x31 -> x10, local copies, waits for them, and re-layouts: 10.3 us -> 2.3 us
    pallas_call x1 -> x0, local copies, waits for them, and re-layouts: 1.75 us -> none  [finish(): pl.pallas_call(functools.partial(finish_kernel, len(parts), taps), out_sh...]
where the time goes in v1:
time: 80.7 us; the launch traced here: 80.3 us
  Pallas kernels  43 us (53%)
  waiting for transfers between devices  26.9 us (33%)
  starting transfers between devices  7.42 us (9%)
  local copies, waits for them, and re-layouts  2.3 us (3%)
    pallas_call x2, Pallas kernels, run_tick(): pl.pallas_call(functools.partial(tick_kernel, last, taps, (len(ins), len(...  41.2 us
    ppermute x3, waiting for transfers between devices, body(): lax.ppermute(message, 'replica', [(i, (i + by) % replicas) for i in range...  14.6 us
    ppermute x1, waiting for transfers between devices, shifted(): return lax.ppermute(array, axis, pairs)  12.3 us
    ppermute x3, starting transfers between devices, body(): lax.ppermute(message, 'replica', [(i, (i + by) % replicas) for i in range...  4.64 us
    ppermute x1, starting transfers between devices, shifted(): return lax.ppermute(array, axis, pairs)  2.78 us
    unnamed x10, local copies, waits for them, and re-layouts  2.3 us
    pallas_call x1, Pallas kernels, finish(): pl.pallas_call(functools.partial(finish_kernel, len(parts), taps), out_sh...  1.85 us
  transfers between devices with their start and end apart: 4, of which 3 were waited for; matrix products, arithmetic and copies ran while one was open for 0% of the time, Pallas kernels for 0%

profile of v1, /device:TPU:4, one launch (start us, length us, event | category | flops | bytes accessed | tf_op | source)
XLA Modules:
  0.0 80.3 jit_solution(12783059972432717454)
XLA Ops:
  0.6 22.6 %first_tick.1 = (bf16[4096,128]{1,0:T(8,128)(2,1)S(1)}, f32[6,256,128]{2,1,0:T(8,128)S(1)}, f32[32,128]{1,0:T(8,128)S(1)}) custom-call(bf16[1,2,1,4096,128]{4,3,2,1,0:T(8,128)(2,1)} %refs_0_.3, bf16[4096,128]{1,0:T(8,128)(2,1)} %bitcast.6, f32[3,7,1,256]{3,2,1,0:T(1,128)} %bitcast.7, f32[1,256,128]{2,1,0:T(8,128)} %refs_3_.3, f32[32,128]{1,0:T(8,128)} %bitcast.9, ...), custom_call_target="tpu_custom_call" | custom-call | tf_op jit(solution)/shard_map/first_tick/pallas_call | solution.py:317
  23.2 2.8 %collective-permute-start = (bf16[4096,128]{1,0:T(8,128)(2,1)S(1)}, bf16[4096,128]{1,0:T(8,128)(2,1)S(1)}, u32[]{:S(2)}, u32[]{:S(2)}) collective-permute-start(bf16[4096,128]{1,0:T(8,128)(2,1)S(1)} %get-tuple-element.9), channel_id=1, source_target_pairs={{4,0},{8,4},{12,8},{16,12},{20,16},{24,20},{28,24},{5,1},{9,5},{13... | collective-permute-start | bytes 3145736 | tf_op jit(solution)/shard_map/ppermute | solution.py:23
  26.0 12.3 %collective-permute-done.refs_1_ = bf16[4096,128]{1,0:T(8,128)(2,1)S(1)} collective-permute-done((bf16[4096,128]{1,0:T(8,128)(2,1)S(1)}, bf16[4096,128]{1,0:T(8,128)(2,1)S(1)}, u32[]{:S(2)}, u32[]{:S(2)}) %collective-permute-start) | collective-permute-done | bytes 1048608 | tf_op jit(solution)/shard_map/ppermute | solution.py:23
  38.3 0.0 copy-start.1
  38.3 1.0 %copy-done.1 = bf16[4096,128]{1,0:T(8,128)(2,1)} copy-done((bf16[4096,128]{1,0:T(8,128)(2,1)}, bf16[4096,128]{1,0:T(8,128)(2,1)S(1)}, u32[]{:S(2)}) %copy-start.1) | copy-done | bytes 1048600
  39.3 18.6 %last_tick.1.refs_0_ = f32[336,128]{1,0:T(8,128)S(1)} custom-call(bf16[1,2,1,4096,128]{4,3,2,1,0:T(8,128)(2,1)} %refs_0_.3, bf16[4096,128]{1,0:T(8,128)(2,1)} %copy-done.1, f32[3,7,1,256]{3,2,1,0:T(1,128)} %bitcast.8, f32[1,256,128]{2,1,0:T(8,128)} %refs_3_.3, f32[32,128]{1,0:T(8,128)} %bitcast.10, bf16[256,256]{1,0:T(8,128)(2,1)} %constant.10.clone.refs_5_, ...), custom_call_target="tpu_custom_call" | custom-call | tf_op jit(solution)/shard_map/last_tick/pallas_call | solution.py:317
  57.9 0.0 copy-start
  57.9 3.6 %collective-permute-start.3 = (f32[336,128]{1,0:T(8,128)S(1)}, f32[336,128]{1,0:T(8,128)S(1)}, u32[]{:S(2)}, u32[]{:S(2)}) collective-permute-start(f32[336,128]{1,0:T(8,128)S(1)} %last_tick.1.refs_0_), channel_id=1, source_target_pairs={{0,3},{1,0},{2,1},{3,2},{4,7},{5,4},{6,5},{7,6},{8,11},{9,8},{10,9... | collective-permute-start | bytes 516104 | tf_op jit(solution)/shard_map/ppermute | solution.py:372
  61.5 0.0 collective-permute-start.2
  61.5 1.0 %collective-permute-start.1 = (f32[336,128]{1,0:T(8,128)S(1)}, f32[336,128]{1,0:T(8,128)S(1)}, u32[]{:S(2)}, u32[]{:S(2)}) collective-permute-start(f32[336,128]{1,0:T(8,128)S(1)} %last_tick.1.refs_0_), channel_id=1, source_target_pairs={{0,1},{1,2},{2,3},{3,0},{4,5},{5,6},{6,7},{7,4},{8,9},{9,10},{10,1... | collective-permute-start | bytes 516104 | tf_op jit(solution)/shard_map/ppermute | solution.py:372
  62.5 3.8 %collective-permute-done.3.refs_3_ = f32[336,128]{1,0:T(8,128)S(1)} collective-permute-done((f32[336,128]{1,0:T(8,128)S(1)}, f32[336,128]{1,0:T(8,128)S(1)}, u32[]{:S(2)}, u32[]{:S(2)}) %collective-permute-start.3) | collective-permute-done | bytes 172064 | tf_op jit(solution)/shard_map/ppermute | solution.py:372
  66.3 0.0 copy-start.2
  66.3 10.8 %collective-permute-done.2.refs_2_ = f32[336,128]{1,0:T(8,128)S(1)} collective-permute-done((f32[336,128]{1,0:T(8,128)S(1)}, f32[336,128]{1,0:T(8,128)S(1)}, u32[]{:S(2)}, u32[]{:S(2)}) %collective-permute-start.2) | collective-permute-done | bytes 172064 | tf_op jit(solution)/shard_map/ppermute | solution.py:372
  77.1 0.0 copy-start.3
  77.1 0.0 collective-permute-done.1.refs_1_
  77.1 0.0 copy-done
  77.1 0.0 copy-done.2
  77.2 0.7 copy-done.3
  77.8 0.0 copy-start.4
  77.8 0.7 copy-done.4
  78.5 1.8 %finish.1 = (f32[3,7,1,256]{3,2,1,0:T(1,128)}, f32[256,128]{1,0:T(8,128)}, f32[32,128]{1,0:T(8,128)}) custom-call(f32[336,128]{1,0:T(8,128)} %copy-done, f32[336,128]{1,0:T(8,128)} %copy-done.4, f32[336,128]{1,0:T(8,128)} %copy-done.3, f32[336,128]{1,0:T(8,128)} %copy-done.2), custom_call_target="tpu_custom_call" | custom-call | tf_op jit(solution)/shard_map/finish/pallas_call | solution.py:348
Async XLA Ops:
  23.2 15.1 %collective-permute-start = (bf16[4096,128]{1,0:T(8,128)(2,1)S(1)}, bf16[4096,128]{1,0:T(8,128)(2,1)S(1)}, u32[]{:S(2)}, u32[]{:S(2)}) collective-permute-start(bf16[4096,128]{1,0:T(8,128)(2,1)S(1)} %get-tuple-element.9), channel_id=1, source_target_pairs={{4,0},{8,4},{12,8},{16,12},{20,16},{24,20},{28,24},{5,1},{9,5},{13... | collective-permute-start | bytes 3145736 | tf_op jit(solution)/shard_map/ppermute | solution.py:23
  38.3 1.0 %copy-start.1 = (bf16[4096,128]{1,0:T(8,128)(2,1)}, bf16[4096,128]{1,0:T(8,128)(2,1)S(1)}, u32[]{:S(2)}) copy-start(bf16[4096,128]{1,0:T(8,128)(2,1)S(1)} %collective-permute-done.refs_1_) | copy-start | bytes 3145732
  57.9 19.3 %copy-start = (f32[336,128]{1,0:T(8,128)}, f32[336,128]{1,0:T(8,128)S(1)}, u32[]{:S(2)}) copy-start(f32[336,128]{1,0:T(8,128)S(1)} %last_tick.1.refs_0_) | copy-start | bytes 516100
  57.9 8.5 %collective-permute-start.3 = (f32[336,128]{1,0:T(8,128)S(1)}, f32[336,128]{1,0:T(8,128)S(1)}, u32[]{:S(2)}, u32[]{:S(2)}) collective-permute-start(f32[336,128]{1,0:T(8,128)S(1)} %last_tick.1.refs_0_), channel_id=1, source_target_pairs={{0,3},{1,0},{2,1},{3,2},{4,7},{5,4},{6,5},{7,6},{8,11},{9,8},{10,9... | collective-permute-start | bytes 516104 | tf_op jit(solution)/shard_map/ppermute | solution.py:372
  61.5 15.7 %collective-permute-start.2 = (f32[336,128]{1,0:T(8,128)S(1)}, f32[336,128]{1,0:T(8,128)S(1)}, u32[]{:S(2)}, u32[]{:S(2)}) collective-permute-start(f32[336,128]{1,0:T(8,128)S(1)} %last_tick.1.refs_0_), channel_id=1, source_target_pairs={{0,2},{1,3},{2,0},{3,1},{4,6},{5,7},{6,4},{7,5},{8,10},{9,11},{10,... | collective-permute-start | bytes 516104 | tf_op jit(solution)/shard_map/ppermute | solution.py:372
  61.5 15.7 %collective-permute-start.1 = (f32[336,128]{1,0:T(8,128)S(1)}, f32[336,128]{1,0:T(8,128)S(1)}, u32[]{:S(2)}, u32[]{:S(2)}) collective-permute-start(f32[336,128]{1,0:T(8,128)S(1)} %last_tick.1.refs_0_), channel_id=1, source_target_pairs={{0,1},{1,2},{2,3},{3,0},{4,5},{5,6},{6,7},{7,4},{8,9},{9,10},{10,1... | collective-permute-start | bytes 516104 | tf_op jit(solution)/shard_map/ppermute | solution.py:372
  66.3 10.8 %copy-start.2 = (f32[336,128]{1,0:T(8,128)}, f32[336,128]{1,0:T(8,128)S(1)}, u32[]{:S(2)}) copy-start(f32[336,128]{1,0:T(8,128)S(1)} %collective-permute-done.3.refs_3_) | copy-start | bytes 516100
  77.1 0.7 copy-start.3
  77.8 0.7 copy-start.4

commit v2 on v1

--- a/solution.py
+++ b/solution.py
@@ -76,7 +76,7 @@
         self.last, self.taps, self.ng = last, taps, SUB // GROUP
         (self.x, self.cot, self.f, self.med, self.skip, self.fwd, self.inv, self.shift) = ins[:8]
         if last:
-            (self.finv, self.acc_in, self.skip_in) = ins[8:]
+            self.finv, self.acc_in, self.skip_in, *self.earlier = ins[8:]
             (self.msg,) = outs
             self.acc, self.skips = scratch[-2:]
         else:
@@ -230,21 +230,20 @@
         total = [self.acc[i] + self.acc_in[i] for i in range(6)]
         real = total[0] + jnp.where(first, 0.0, total[1])
         imag = jnp.where(first, total[1], total[2])
-        at = real.shape[0]
         both = jnp.concatenate([real, imag], axis=1)
-        self.msg[:at] = mm(both, self.finv[...], PRECISE)
-        count = self.skips.shape[0]
-        self.msg[at : at + count] = self.skips[...] + self.skip_in[...]
-        at += count
         pick = (
             lax.broadcasted_iota(jnp.int32, (8, LANES), 1) // GROUP
             == lax.broadcasted_iota(jnp.int32, (8, LANES), 0)
         ).astype(F32)
-        for m in range(3):
-            for q in range(real.shape[0] // LANES):
-                part = total[3 + m][LANES * q : LANES * (q + 1)]
-                self.msg[at : at + 8] = nt(pick, part, PRECISE)
-                at += 8
+        pieces = [mm(both, self.finv[...], PRECISE), self.skips[...] + self.skip_in[...]]
+        pieces += [nt(pick, total[3 + m], PRECISE) for m in range(3)]
+        pieces.append(jnp.zeros((8, LANES), F32))
+        mine = jnp.concatenate(pieces, axis=0).astype(BF16)
+        at = 0
+        for ref in self.earlier:
+            self.msg[: ref.shape[0]] = ref[...]
+            at = ref.shape[0]
+        self.msg[at : at + mine.shape[0]] = mine
 
 
 def tick_kernel(last, taps, counts, *refs):
@@ -271,19 +270,27 @@
     return pltpu.with_memory_space_constraint(array, pltpu.HBM)
 
 
-def run_tick(saved, cot, filters, medium, skip_rows, tick, prior):
+def run_tick(saved, cot, filters, medium, skip_rows, tick, chunk, chunks, prior):
     last = prior is not None
-    channels, length = saved.shape[-2:]
+    total, length = saved.shape[-2:]
+    channels = total // chunks
     taps = filters.shape[1]
-    groups = filters.shape[3]
+    groups = channels // GROUP
     forward, inverse, inverse_full, shift, unshift = tables(length, taps)
     ng = SUB // GROUP
-    full = lambda a: pl.BlockSpec(a.shape, lambda i: (0,) * a.ndim)
-    x_spec = pl.BlockSpec((1, 1, 1, channels, length), lambda i: (0, tick, 0, 0, 0))
+    full = lambda a: pl.BlockSpec(a.shape, lambda i: (0,) * len(a.shape))
+    at = chunk if cot.shape[0] == total else 0
     ins = [saved, cot, filters, medium, skip_rows, forward, inverse, shift]
     ins += [inverse_full] if last else [unshift]
-    ins = [in_hbm(jnp.asarray(a)) for a in ins]
+    ins = [a if last and a is cot else in_hbm(jnp.asarray(a)) for a in ins]
     ins += [*prior] if last else []
+    in_specs = [
+        pl.BlockSpec((1, 1, 1, channels, length), lambda i: (0, tick, 0, chunk, 0)),
+        pl.BlockSpec((channels, length), lambda i: (at, 0)),
+        pl.BlockSpec((3, taps, 1, groups), lambda i: (0, 0, 0, chunk)),
+        pl.BlockSpec((1, groups, length), lambda i: (0, chunk, 0)),
+        pl.BlockSpec((channels // LANES, LANES), lambda i: (chunk, 0)),
+    ] + [full(a) for a in ins[5:]]
     acc_shape = (6, groups, LANES)
     skip_shape = (channels // LANES, LANES)
     slot = [
@@ -306,7 +313,8 @@
         pltpu.VMEM((LANES, LANES), F32),
     ]
     if last:
-        outs = [jax.ShapeDtypeStruct((groups + channels // LANES + 24 * (groups // LANES), LANES), F32)]
+        rows = (groups + channels // LANES + 32) * (chunk + 1)
+        outs = [jax.ShapeDtypeStruct((rows, LANES), BF16)]
         scratch += [pltpu.VMEM(acc_shape, F32), pltpu.VMEM(skip_shape, F32)]
     else:
         outs = [
@@ -318,7 +326,7 @@
         functools.partial(tick_kernel, last, taps, (len(ins), len(outs))),
         out_shape=outs,
         grid=(1,),
-        in_specs=[x_spec] + [full(a) for a in ins[1:]],
+        in_specs=in_specs,
         out_specs=[full(a) for a in outs],
         scratch_shapes=scratch,
         compiler_params=pltpu.CompilerParams(vmem_limit_bytes=48 << 20),
@@ -326,53 +334,65 @@
     )(*ins)
 
 
-def finish_kernel(count, taps, *refs):
+def finish_kernel(count, taps, chunks, *refs):
     ins, (short_ref, medium_ref, skip_ref) = refs[:count], refs[count:]
-    total = ins[0][...]
+    total = ins[0][...].astype(F32)
     for ref in ins[1:]:
-        total = total + ref[...]
+        total = total + ref[...].astype(F32)
     total = total * (1.0 / count)
-    groups = medium_ref.shape[0]
-    medium_ref[...] = total[:groups]
-    at = groups + skip_ref.shape[0]
-    skip_ref[...] = total[groups:at]
-    for m in range(3):
-        for q in range(groups // LANES):
+    groups = medium_ref.shape[0] // chunks
+    skips = skip_ref.shape[0] // chunks
+    for c in range(chunks):
+        at = c * (total.shape[0] // chunks)
+        medium_ref[groups * c : groups * (c + 1)] = total[at : at + groups]
+        at += groups
+        skip_ref[skips * c : skips * (c + 1)] = total[at : at + skips]
+        at += skips
+        for m in range(3):
             for j in range(taps):
-                short_ref[m, j, :, LANES * q : LANES * (q + 1)] = total[at + j : at + j + 1]
+                short_ref[m, j, :, groups * c : groups * (c + 1)] = total[at + j : at + j + 1]
             at += 8
 
 
-def finish(parts, groups, channels, taps):
-    vmem = pl.BlockSpec(memory_space=pltpu.VMEM)
+def finish(parts, groups, channels, taps, chunks):
+    full = lambda a: pl.BlockSpec(a.shape, lambda i: (0,) * len(a.shape))
+    outs = (
+        jax.ShapeDtypeStruct((3, taps, 1, groups), F32),
+        jax.ShapeDtypeStruct((groups, LANES), F32),
+        jax.ShapeDtypeStruct((channels // LANES, LANES), F32),
+    )
     return pl.pallas_call(
-        functools.partial(finish_kernel, len(parts), taps),
-        out_shape=(
-            jax.ShapeDtypeStruct((3, taps, 1, groups), F32),
-            jax.ShapeDtypeStruct((groups, LANES), F32),
-            jax.ShapeDtypeStruct((channels // LANES, LANES), F32),
-        ),
-        in_specs=[vmem] * len(parts),
-        out_specs=[vmem] * 3,
+        functools.partial(finish_kernel, len(parts), taps, chunks),
+        out_shape=outs,
+        grid=(1,),
+        in_specs=[full(a) for a in parts],
+        out_specs=tuple(full(a) for a in outs),
+        compiler_params=pltpu.CompilerParams(vmem_limit_bytes=8 << 20),
         name="finish",
     )(*parts)
 
 
 def body(saved, upstream, short_filters, medium_filter, skip):
-    channels, length = saved.shape[-2:]
+    channels = saved.shape[-2]
     groups, taps = short_filters.shape[2:]
     replicas = lax.axis_size("replica")
+    chunks = groups // LANES
     skip_rows = skip.reshape(channels // LANES, LANES)
     filters = jnp.transpose(short_filters, (1, 3, 0, 2))
-    incoming = upstream[0, 0]
-    gin, acc, skips = run_tick(saved, incoming, filters, medium_filter, skip_rows, 0, None)
-    incoming = shifted(gin, "section", -1)
-    (message,) = run_tick(saved, incoming, filters, medium_filter, skip_rows, 1, (acc, skips))
-    parts = [message] + [
-        lax.ppermute(message, "replica", [(i, (i + by) % replicas) for i in range(replicas)])
+    rest = (filters, medium_filter, skip_rows)
+    incoming, prior = [], []
+    for c in range(chunks):
+        gin, *sums = run_tick(saved, upstream[0, 0], *rest, 0, c, chunks, None)
+        incoming.append(shifted(gin, "section", -1))
+        prior.append(sums)
+    message = []
+    for c in range(chunks):
+        message = run_tick(saved, incoming[c], *rest, 1, c, chunks, (*prior[c], *message))
+    parts = [*message] + [
+        lax.ppermute(message[0], "replica", [(i, (i + by) % replicas) for i in range(replicas)])
         for by in range(1, replicas)
     ]
-    short, medium, skip_grad = finish(parts, groups, channels, taps)
+    short, medium, skip_grad = finish(parts, groups, channels, taps, chunks)
     return (
         jnp.transpose(short, (2, 0, 3, 1)),
         medium[None],

time: 80.7 us -> 63.5 us (0.79)
  waiting for transfers between devices: 26.9 us -> 7.11 us
  starting transfers between devices: 7.42 us -> 10 us
  Pallas kernels: 43 us -> 45.5 us
  local copies, waits for them, and re-layouts: 2.3 us -> 0 us
    ppermute x1 -> x2, waiting for transfers between devices: 12.3 us -> 0.01 us  [shifted(): return lax.ppermute(array, axis, pairs)]
    ppermute x3, waiting for transfers between devices: 14.6 us -> 7.11 us  [body(): lax.ppermute(message[0], 'replica', [(i, (i + by) % replicas) for i in ra...]
    pallas_call x2 -> x4, Pallas kernels: 41.2 us -> 44.8 us  [run_tick(): pl.pallas_call(functools.partial(tick_kernel, last, taps, (len(ins), len(...]
    ppermute x1 -> x2, starting transfers between devices: 2.78 us -> 5.38 us  [shifted(): return lax.ppermute(array, axis, pairs)]
    unnamed x10 -> x0, local copies, waits for them, and re-layouts: 2.3 us -> none
    pallas_call x1, Pallas kernels: 1.85 us -> 0.7 us  [finish(): pl.pallas_call(functools.partial(finish_kernel, len(parts), taps, chunks)...]
  transfers between devices with their start and end apart: 4 -> 5, of which waited for: 3 -> 2; matrix products, arithmetic and copies ran while one was open for 0% -> 0% of each run, Pallas kernels for 0% -> 35%
where the time goes in v2:
time: 63.5 us; the launch traced here: 63.3 us
  Pallas kernels  45.5 us (72%)
  starting transfers between devices  10 us (16%)
  waiting for transfers between devices  7.11 us (11%)
  between operations  0.67 us (1%)
    pallas_call x4, Pallas kernels, run_tick(): pl.pallas_call(functools.partial(tick_kernel, last, taps, (len(ins), len(...  44.8 us
    ppermute x3, waiting for transfers between devices, body(): lax.ppermute(message[0], 'replica', [(i, (i + by) % replicas) for i in ra...  7.11 us
    ppermute x2, starting transfers between devices, shifted(): return lax.ppermute(array, axis, pairs)  5.38 us
    ppermute x3, starting transfers between devices, body(): lax.ppermute(message[0], 'replica', [(i, (i + by) % replicas) for i in ra...  4.65 us
  transfers between devices with their start and end apart: 5, of which 2 were waited for; matrix products, arithmetic and copies ran while one was open for 0% of the time, Pallas kernels for 35%

profile of v2, /device:TPU:4, one launch (start us, length us, event | category | flops | bytes accessed | tf_op | source)
XLA Modules:
  0.0 63.3 jit_solution(9449543378450351971)
XLA Ops:
  0.6 12.1 %first_tick.3 = (bf16[2048,128]{1,0:T(8,128)(2,1)S(1)}, f32[6,128,128]{2,1,0:T(8,128)S(1)}, f32[16,128]{1,0:T(8,128)S(1)}) custom-call(bf16[1,2,1,4096,128]{4,3,2,1,0:T(8,128)(2,1)} %refs_0_.7, bf16[4096,128]{1,0:T(8,128)(2,1)} %bitcast.6, f32[3,7,1,256]{3,2,1,0:T(1,128)} %bitcast.8, f32[1,256,128]{2,1,0:T(8,128)} %refs_3_.7, f32[32,128]{1,0:T(8,128)} %bitcast.12, ...), custom_call_target="tpu_custom_call" | custom-call | tf_op jit(solution)/shard_map/first_tick/pallas_call | solution.py:325
  12.8 2.8 %collective-permute-start.1 = (bf16[2048,128]{1,0:T(8,128)(2,1)S(1)}, bf16[2048,128]{1,0:T(8,128)(2,1)S(1)}, u32[]{:S(2)}, u32[]{:S(2)}) collective-permute-start(bf16[2048,128]{1,0:T(8,128)(2,1)S(1)} %get-tuple-element.15), channel_id=1, source_target_pairs={{4,0},{8,4},{12,8},{16,12},{20,16},{24,20},{28,24},{5,1},{9,5},{13... | collective-permute-start | bytes 1572872 | tf_op jit(solution)/shard_map/ppermute | solution.py:23
  15.5 12.1 %first_tick.2 = (bf16[2048,128]{1,0:T(8,128)(2,1)S(1)}, f32[6,128,128]{2,1,0:T(8,128)S(1)}, f32[16,128]{1,0:T(8,128)S(1)}) custom-call(bf16[1,2,1,4096,128]{4,3,2,1,0:T(8,128)(2,1)} %refs_0_.7, bf16[4096,128]{1,0:T(8,128)(2,1)} %bitcast.7, f32[3,7,1,256]{3,2,1,0:T(1,128)} %bitcast.9, f32[1,256,128]{2,1,0:T(8,128)} %refs_3_.7, f32[32,128]{1,0:T(8,128)} %bitcast.13, ...), custom_call_target="tpu_custom_call" | custom-call | tf_op jit(solution)/shard_map/first_tick/pallas_call | solution.py:325
  27.7 2.6 %collective-permute-start = (bf16[2048,128]{1,0:T(8,128)(2,1)S(1)}, bf16[2048,128]{1,0:T(8,128)(2,1)S(1)}, u32[]{:S(2)}, u32[]{:S(2)}) collective-permute-start(bf16[2048,128]{1,0:T(8,128)(2,1)S(1)} %get-tuple-element.12), channel_id=1, source_target_pairs={{4,0},{8,4},{12,8},{16,12},{20,16},{24,20},{28,24},{5,1},{9,5},{13... | collective-permute-start | bytes 1572872 | tf_op jit(solution)/shard_map/ppermute | solution.py:23
  30.3 0.0 collective-permute-done.1.refs_1_
  30.3 10.3 %last_tick.2.refs_11_ = bf16[176,128]{1,0:T(8,128)(2,1)S(1)} custom-call(bf16[1,2,1,4096,128]{4,3,2,1,0:T(8,128)(2,1)} %refs_0_.7, bf16[2048,128]{1,0:T(8,128)(2,1)S(1)} %collective-permute-done.1.refs_1_, f32[3,7,1,256]{3,2,1,0:T(1,128)} %bitcast.10, f32[1,256,128]{2,1,0:T(8,128)} %refs_3_.7, f32[32,128]{1,0:T(8,128)} %bitcast.14, ...), custom_call_target="tpu_custom_call" | custom-call | tf_op jit(solution)/shard_map/last_tick/pallas_call | solution.py:325
  40.5 0.0 collective-permute-done.refs_1_
  40.6 10.3 %last_tick.3.refs_0_ = bf16[352,128]{1,0:T(8,128)(2,1)S(1)} custom-call(bf16[1,2,1,4096,128]{4,3,2,1,0:T(8,128)(2,1)} %refs_0_.7, bf16[2048,128]{1,0:T(8,128)(2,1)S(1)} %collective-permute-done.refs_1_, f32[3,7,1,256]{3,2,1,0:T(1,128)} %bitcast.11, f32[1,256,128]{2,1,0:T(8,128)} %refs_3_.7, f32[32,128]{1,0:T(8,128)} %bitcast.15, ...), custom_call_target="tpu_custom_call" | custom-call | tf_op jit(solution)/shard_map/last_tick/pallas_call | solution.py:325
  50.8 3.6 %collective-permute-start.4 = (bf16[352,128]{1,0:T(8,128)(2,1)S(1)}, bf16[352,128]{1,0:T(8,128)(2,1)S(1)}, u32[]{:S(2)}, u32[]{:S(2)}) collective-permute-start(bf16[352,128]{1,0:T(8,128)(2,1)S(1)} %last_tick.3.refs_0_), channel_id=1, source_target_pairs={{0,3},{1,0},{2,1},{3,2},{4,7},{5,4},{6,5},{7,6},{8,11},{9,8},{10,9... | collective-permute-start | bytes 270344 | tf_op jit(solution)/shard_map/ppermute | solution.py:392
  54.5 0.0 collective-permute-start.3
  54.5 1.0 %collective-permute-start.2 = (bf16[352,128]{1,0:T(8,128)(2,1)S(1)}, bf16[352,128]{1,0:T(8,128)(2,1)S(1)}, u32[]{:S(2)}, u32[]{:S(2)}) collective-permute-start(bf16[352,128]{1,0:T(8,128)(2,1)S(1)} %last_tick.3.refs_0_), channel_id=1, source_target_pairs={{0,1},{1,2},{2,3},{3,0},{4,5},{5,6},{6,7},{7,4},{8,9},{9,10},{10,1... | collective-permute-start | bytes 270344 | tf_op jit(solution)/shard_map/ppermute | solution.py:392
  55.5 2.0 %collective-permute-done.4.refs_3_ = bf16[352,128]{1,0:T(8,128)(2,1)S(1)} collective-permute-done((bf16[352,128]{1,0:T(8,128)(2,1)S(1)}, bf16[352,128]{1,0:T(8,128)(2,1)S(1)}, u32[]{:S(2)}, u32[]{:S(2)}) %collective-permute-start.4) | collective-permute-done | bytes 90144 | tf_op jit(solution)/shard_map/ppermute | solution.py:392
  57.5 5.1 %collective-permute-done.3.refs_2_ = bf16[352,128]{1,0:T(8,128)(2,1)S(1)} collective-permute-done((bf16[352,128]{1,0:T(8,128)(2,1)S(1)}, bf16[352,128]{1,0:T(8,128)(2,1)S(1)}, u32[]{:S(2)}, u32[]{:S(2)}) %collective-permute-start.3) | collective-permute-done | bytes 90144 | tf_op jit(solution)/shard_map/ppermute | solution.py:392
  62.6 0.0 collective-permute-done.2.refs_1_
  62.6 0.7 %finish.1 = (f32[3,7,1,256]{3,2,1,0:T(1,128)}, f32[256,128]{1,0:T(8,128)}, f32[32,128]{1,0:T(8,128)}) custom-call(bf16[352,128]{1,0:T(8,128)(2,1)S(1)} %last_tick.3.refs_0_, bf16[352,128]{1,0:T(8,128)(2,1)S(1)} %collective-permute-done.2.refs_1_, bf16[352,128]{1,0:T(8,128)(2,1)S(1)} %collective-permute-done.3.refs_2_, ...), custom_call_target="tpu_custom_call" | custom-call | tf_op jit(solution)/shard_map/finish/pallas_call | solution.py:364
Async XLA Ops:
  12.8 17.5 %collective-permute-start.1 = (bf16[2048,128]{1,0:T(8,128)(2,1)S(1)}, bf16[2048,128]{1,0:T(8,128)(2,1)S(1)}, u32[]{:S(2)}, u32[]{:S(2)}) collective-permute-start(bf16[2048,128]{1,0:T(8,128)(2,1)S(1)} %get-tuple-element.15), channel_id=1, source_target_pairs={{4,0},{8,4},{12,8},{16,12},{20,16},{24,20},{28,24},{5,1},{9,5},{13... | collective-permute-start | bytes 1572872 | tf_op jit(solution)/shard_map/ppermute | solution.py:23
  27.7 12.9 %collective-permute-start = (bf16[2048,128]{1,0:T(8,128)(2,1)S(1)}, bf16[2048,128]{1,0:T(8,128)(2,1)S(1)}, u32[]{:S(2)}, u32[]{:S(2)}) collective-permute-start(bf16[2048,128]{1,0:T(8,128)(2,1)S(1)} %get-tuple-element.12), channel_id=1, source_target_pairs={{4,0},{8,4},{12,8},{16,12},{20,16},{24,20},{28,24},{5,1},{9,5},{13... | collective-permute-start | bytes 1572872 | tf_op jit(solution)/shard_map/ppermute | solution.py:23
  50.8 6.7 %collective-permute-start.4 = (bf16[352,128]{1,0:T(8,128)(2,1)S(1)}, bf16[352,128]{1,0:T(8,128)(2,1)S(1)}, u32[]{:S(2)}, u32[]{:S(2)}) collective-permute-start(bf16[352,128]{1,0:T(8,128)(2,1)S(1)} %last_tick.3.refs_0_), channel_id=1, source_target_pairs={{0,3},{1,0},{2,1},{3,2},{4,7},{5,4},{6,5},{7,6},{8,11},{9,8},{10,9... | collective-permute-start | bytes 270344 | tf_op jit(solution)/shard_map/ppermute | solution.py:392
  54.5 8.1 %collective-permute-start.3 = (bf16[352,128]{1,0:T(8,128)(2,1)S(1)}, bf16[352,128]{1,0:T(8,128)(2,1)S(1)}, u32[]{:S(2)}, u32[]{:S(2)}) collective-permute-start(bf16[352,128]{1,0:T(8,128)(2,1)S(1)} %last_tick.3.refs_0_), channel_id=1, source_target_pairs={{0,2},{1,3},{2,0},{3,1},{4,6},{5,7},{6,4},{7,5},{8,10},{9,11},{10,... | collective-permute-start | bytes 270344 | tf_op jit(solution)/shard_map/ppermute | solution.py:392
  54.5 8.1 %collective-permute-start.2 = (bf16[352,128]{1,0:T(8,128)(2,1)S(1)}, bf16[352,128]{1,0:T(8,128)(2,1)S(1)}, u32[]{:S(2)}, u32[]{:S(2)}) collective-permute-start(bf16[352,128]{1,0:T(8,128)(2,1)S(1)} %last_tick.3.refs_0_), channel_id=1, source_target_pairs={{0,1},{1,2},{2,3},{3,0},{4,5},{5,6},{6,7},{7,4},{8,9},{9,10},{10,1... | collective-permute-start | bytes 270344 | tf_op jit(solution)/shard_map/ppermute | solution.py:392

commit v3 on v2

--- a/solution.py
+++ b/solution.py
@@ -11,6 +11,7 @@
 GROUP = 16
 LANES = 128
 SUB = 128
+RING = 4
 
 F32 = jnp.float32
 BF16 = jnp.bfloat16
@@ -75,16 +76,18 @@
     def __init__(self, last, taps, ins, outs, scratch):
         self.last, self.taps, self.ng = last, taps, SUB // GROUP
         (self.x, self.cot, self.f, self.med, self.skip, self.fwd, self.inv, self.shift) = ins[:8]
+        scratch = list(scratch)
         if last:
             self.finv, self.acc_in, self.skip_in, *self.earlier = ins[8:]
             (self.msg,) = outs
-            self.acc, self.skips = scratch[-2:]
+            self.acc, self.skips = scratch.pop(0), scratch.pop(0)
         else:
             (self.unshift,) = ins[8:]
             self.gin, self.acc, self.skips = outs
-        self.columns, self.coef = scratch[:2]
-        self.slots = (scratch[2:9], scratch[9:16])
-        self.spec, self.res, self.red, self.sums, self.hats, self.turn = scratch[16:22]
+        self.columns, self.coef, self.turn = scratch[:3]
+        rings = [scratch[i : i + RING] for i in range(3, len(scratch), RING)]
+        (self.taps_at, self.coef_at, self.skip_at, self.xs, self.feat, self.lows, self.hat,
+         self.spec, self.res, self.terms, self.sums, self.hats, self.corr) = rings
 
     def rows(self, block):
         return pl.multiple_of(block * SUB, SUB)
@@ -110,7 +113,7 @@
             self.columns[cols, :] = self.turn[...].T
 
     def start(self, block, slot):
-        taps_at, coef_at, skip_at, xs, _, _, _ = self.slots[slot]
+        taps_at, skip_at, xs = self.taps_at[slot], self.skip_at[slot], self.xs[slot]
         x = self.x[0, 0, 0, pl.ds(self.rows(block), SUB), :]
         xs[:, LANES:] = mm(x, self.shift[...])
         xs[:, :LANES] = x.astype(F32)
@@ -118,11 +121,13 @@
         for t in range(3 * self.taps):
             taps_at[t] = jnp.broadcast_to(mine[:, t : t + 1], (self.ng, LANES))
         for i in range(3):
-            coef_at[i] = self.coef[i, self.groups(block), :]
-        skip_at[...] = jnp.broadcast_to(self.skip[pl.ds(block, 1), :], (SUB, LANES)).T
+            self.coef_at[slot][i] = self.coef[i, self.groups(block), :]
+        for q in range(SUB // LANES):
+            skip = self.skip[pl.ds(block * (SUB // LANES) + q, 1), :]
+            skip_at[LANES * q : LANES * (q + 1)] = jnp.broadcast_to(skip, (LANES, LANES)).T
 
     def features(self, block, slot):
-        taps_at, _, _, xs, feat, lows, _ = self.slots[slot]
+        taps_at, xs, feat, lows = (r[slot] for r in (self.taps_at, self.xs, self.feat, self.lows))
         for k in range(self.ng):
             r = slice(GROUP * k, GROUP * (k + 1))
             rg = slice(SUB + GROUP * k, SUB + GROUP * (k + 1))
@@ -142,15 +147,13 @@
             feat[3, r] = gm
             lows[r] = product.astype(BF16)
             lows[rg] = gm.astype(BF16)
-
-    def spectra(self, slot):
-        lows, hat = self.slots[slot][5:]
         low = lows[...]
-        hat[...] = mm(jnp.concatenate([low, low], axis=1), self.fwd[...])
+        self.hat[slot][...] = mm(jnp.concatenate([low, low], axis=1), self.fwd[...])
 
     def filter(self, slot):
-        _, coef_at, _, _, _, _, hat = self.slots[slot]
-        spec, red = self.spec, self.red
+        coef_at, hat, spec, terms = (
+            r[slot] for r in (self.coef_at, self.hat, self.spec, self.terms)
+        )
         for k in range(self.ng):
             r = slice(GROUP * k, GROUP * (k + 1))
             rg = slice(SUB + GROUP * k, SUB + GROUP * (k + 1))
@@ -162,68 +165,86 @@
             spec[rg, :LANES] = (gr * ca + gi * cb).astype(BF16)
             spec[rg, LANES:] = (gi * cc - gr * cb).astype(BF16)
             for i, value in enumerate((pr * gr, pi * gi, pr * gi - pi * gr)):
-                red[i, 8 * k : 8 * k + 8, :] = value[:8] + value[8:]
-
-    def invert(self):
-        both = self.spec[...]
-        self.res[...] = mm(jnp.concatenate([both, both], axis=1), self.inv[...])
+                terms[i, 8 * k : 8 * k + 8, :] = value[:8] + value[8:]
+        both = spec[...]
+        self.res[slot][...] = mm(jnp.concatenate([both, both], axis=1), self.inv[...])
 
     def gradients(self, block, slot):
-        taps_at, _, skip_at, xs, feat, _, _ = self.slots[slot]
-        own = own_channel()
+        taps_at, skip_at, xs, feat, res, sums, hats, corr = (
+            r[slot]
+            for r in (self.taps_at, self.skip_at, self.xs, self.feat, self.res, self.sums,
+                      self.hats, self.corr)
+        )
         for k in range(self.ng):
             r = slice(GROUP * k, GROUP * (k + 1))
             rg = slice(SUB + GROUP * k, SUB + GROUP * (k + 1))
             cot = self.cot[pl.ds(self.rows(block) + GROUP * k, GROUP), :].astype(F32)
             kf, vf, product, gm = (feat[i, r] for i in range(4))
             sk = skip_at[r]
-            gq = cot * (self.res[r] + sk * product)
-            gp = self.res[rg] + sk * gm
+            gq = cot * (res[r] + sk * product)
+            gp = res[rg] + sk * gm
             gf = [gq, gp * vf, gp * kf]
-            self.sums[r] = (gm * product).astype(BF16)
+            sums[r] = (gm * product).astype(BF16)
             gfb = jnp.concatenate([g.astype(BF16) for g in gf], axis=0)
             xsb = jnp.concatenate(
                 [xs[r, LANES * j : LANES * (j + 1)].astype(BF16) for j in range(self.taps)]
                 + [jnp.zeros((GROUP, LANES), BF16)] * (LANES // GROUP - self.taps),
                 axis=0,
             )
-            corr = nt(gfb, xsb)
+            corr[k] = nt(gfb, xsb)
             if not self.last:
                 for j in range(self.taps):
                     total = None
                     for m in range(3):
                         tap = row(taps_at, m * self.taps + j, slice(k, k + 1))
                         total = tap * gf[m] if total is None else total + tap * gf[m]
-                    self.hats[r, LANES * j : LANES * (j + 1)] = total.astype(BF16)
+                    hats[r, LANES * j : LANES * (j + 1)] = total.astype(BF16)
+
+    def finish(self, block, slot):
+        terms, corr = self.terms[slot], self.corr[slot]
+        own = own_channel()
+        for k in range(self.ng):
             for m in range(3):
-                kept = jnp.where(own, corr[GROUP * m : GROUP * (m + 1)], 0.0)
-                self.red[3 + m, 8 * k : 8 * k + 8, :] = kept[:8] + kept[8:]
-
-    def reduce(self, block, terms):
-        for i in terms:
-            total = self.red[i, pl.ds(0, self.ng, stride=8), :]
+                kept = jnp.where(own, corr[k, GROUP * m : GROUP * (m + 1)], 0.0)
+                terms[3 + m, 8 * k : 8 * k + 8, :] = kept[:8] + kept[8:]
+        for i in range(6):
+            total = terms[i, pl.ds(0, self.ng, stride=8), :]
             for s in range(1, 8):
-                total = total + self.red[i, pl.ds(s, self.ng, stride=8), :]
+                total = total + terms[i, pl.ds(s, self.ng, stride=8), :]
             self.acc[i, self.groups(block), :] = total
-
-    def finish(self, block):
         if not self.last:
             rows = pl.ds(self.rows(block), SUB)
-            gin = mm(self.hats[...], self.unshift[...]) + self.cot[rows, :].astype(F32)
+            gin = mm(self.hats[slot][...], self.unshift[...]) + self.cot[rows, :].astype(F32)
             self.gin[rows, :] = gin.astype(BF16)
-        self.skips[pl.ds(block, 1), :] = nt(jnp.ones((8, LANES), BF16), self.sums[...])[:1]
-        self.reduce(block, range(3, 6))
-
-    def step(self, block, blocks, slot):
-        after = jnp.minimum(block + 1, blocks - 1)
-        self.start(after, 1 - slot)
-        self.filter(slot)
-        self.invert()
-        self.finish(jnp.maximum(block - 1, 0))
-        self.features(after, 1 - slot)
-        self.reduce(block, range(3))
-        self.spectra(1 - slot)
-        self.gradients(block, slot)
+        sums = nt(jnp.ones((8, LANES), BF16), self.sums[slot][...])
+        for q in range(SUB // LANES):
+            at = pl.ds(block * (SUB // LANES) + q, 1)
+            self.skips[at, :] = sums[:1, LANES * q : LANES * (q + 1)]
+
+    def run(self, blocks):
+        for t in range(3):
+            self.start(t, t % RING)
+        for t in range(2):
+            self.features(t, t % RING)
+        self.filter(0)
+
+        def turn(index, _):
+            for u in range(RING):
+                t = RING * index + u
+                stages = {
+                    "a": (self.start, jnp.minimum(t + 3, blocks - 1), (u + 3) % RING),
+                    "b": (self.features, jnp.minimum(t + 2, blocks - 1), (u + 2) % RING),
+                    "c": (self.filter, (u + 1) % RING),
+                    "d": (self.gradients, t, u),
+                    "e": (self.finish, jnp.maximum(t - 1, 0), (u - 1) % RING),
+                }
+                for name in "aecbd" if self.last else "cadbe":
+                    stage, *where = stages[name]
+                    stage(*where)
+            return 0
+
+        lax.fori_loop(0, blocks // RING, turn, 0)
+        self.finish(blocks - 1, (blocks - 1) % RING)
 
     def message(self):
         first = lax.broadcasted_iota(jnp.int32, (1, LANES), 1) == 0
@@ -251,17 +272,7 @@
     tick = Tick(last, taps, ins, outs, scratch)
     blocks = tick.x.shape[-2] // SUB
     tick.setup()
-    tick.start(0, 0)
-    tick.features(0, 0)
-    tick.spectra(0)
-
-    def pair(index, _):
-        tick.step(2 * index, blocks, 0)
-        tick.step(2 * index + 1, blocks, 1)
-        return 0
-
-    lax.fori_loop(0, blocks // 2, pair, 0)
-    tick.finish(blocks - 1)
+    tick.run(blocks)
     if last:
         tick.message()
 
@@ -282,7 +293,8 @@
     at = chunk if cot.shape[0] == total else 0
     ins = [saved, cot, filters, medium, skip_rows, forward, inverse, shift]
     ins += [inverse_full] if last else [unshift]
-    ins = [a if last and a is cot else in_hbm(jnp.asarray(a)) for a in ins]
+    if not last and chunk == 0:
+        ins = [in_hbm(jnp.asarray(a)) for a in ins]
     ins += [*prior] if last else []
     in_specs = [
         pl.BlockSpec((1, 1, 1, channels, length), lambda i: (0, tick, 0, chunk, 0)),
@@ -293,7 +305,7 @@
     ] + [full(a) for a in ins[5:]]
     acc_shape = (6, groups, LANES)
     skip_shape = (channels // LANES, LANES)
-    slot = [
+    ring = [
         pltpu.VMEM((3 * taps, ng, LANES), F32),
         pltpu.VMEM((3, ng, LANES), F32),
         pltpu.VMEM((SUB, LANES), F32),
@@ -301,21 +313,23 @@
         pltpu.VMEM((4, SUB, LANES), F32),
         pltpu.VMEM((2 * SUB, LANES), BF16),
         pltpu.VMEM((2 * SUB, 2 * LANES), F32),
-    ]
-    scratch = [pltpu.VMEM((groups, LANES), F32), pltpu.VMEM((3, groups, LANES), F32)]
-    scratch += slot + slot
-    scratch += [
         pltpu.VMEM((2 * SUB, 2 * LANES), BF16),
         pltpu.VMEM((2 * SUB, LANES), F32),
         pltpu.VMEM((6, 8 * ng, LANES), F32),
         pltpu.VMEM((SUB, LANES), BF16),
         pltpu.VMEM((SUB, taps * LANES), BF16),
+        pltpu.VMEM((ng, 3 * GROUP, LANES), F32),
+    ]
+    scratch = [pltpu.VMEM(acc_shape, F32), pltpu.VMEM(skip_shape, F32)] if last else []
+    scratch += [
+        pltpu.VMEM((groups, LANES), F32),
+        pltpu.VMEM((3, groups, LANES), F32),
         pltpu.VMEM((LANES, LANES), F32),
     ]
+    scratch += [ref for ref in ring for _ in range(RING)]
     if last:
         rows = (groups + channels // LANES + 32) * (chunk + 1)
         outs = [jax.ShapeDtypeStruct((rows, LANES), BF16)]
-        scratch += [pltpu.VMEM(acc_shape, F32), pltpu.VMEM(skip_shape, F32)]
     else:
         outs = [
             jax.ShapeDtypeStruct((channels, length), BF16),

time: 63.5 us -> 57.4 us (0.904); the launches traced: 63.3 us -> 56.3 us
  Pallas kernels: 45.5 us -> 38.1 us
    pallas_call x4, Pallas kernels: 44.8 us -> 37.4 us  [run_tick(): pl.pallas_call(functools.partial(tick_kernel, last, taps, (len(ins), len(...]
  transfers between devices with their start and end apart: 5 -> 5, of which waited for: 2 -> 2; matrix products, arithmetic and copies ran while one was open for 0% -> 0% of each run, Pallas kernels for 35% -> 32%
where the time goes in v3:
time: 57.4 us; the launch traced here: 56.3 us
  Pallas kernels  38.1 us (66%)
  starting transfers between devices  10.1 us (18%)
  waiting for transfers between devices  7.13 us (12%)
  between operations  0.83 us (1%)
    pallas_call x4, Pallas kernels, run_tick(): pl.pallas_call(functools.partial(tick_kernel, last, taps, (len(ins), len(...  37.4 us
    ppermute x3, waiting for transfers between devices, body(): lax.ppermute(message[0], 'replica', [(i, (i + by) % replicas) for i in ra...  7.12 us
    ppermute x2, starting transfers between devices, shifted(): return lax.ppermute(array, axis, pairs)  5.5 us
    ppermute x3, starting transfers between devices, body(): lax.ppermute(message[0], 'replica', [(i, (i + by) % replicas) for i in ra...  4.64 us
  transfers between devices with their start and end apart: 5, of which 2 were waited for; matrix products, arithmetic and copies ran while one was open for 0% of the time, Pallas kernels for 32%

profile of v3, /device:TPU:4, one launch (start us, length us, event | category | flops | bytes accessed | tf_op | source)
XLA Modules:
  0.0 56.3 jit_solution(751123984919775469)
XLA Ops:
  0.6 0.0 copy-start.2
  0.6 0.0 copy-start.4
  0.7 0.0 copy-start.5
  0.7 0.0 copy-start.6
  0.7 0.0 copy-start.3
  0.7 0.0 copy-start
  0.7 0.0 copy-start.9
  0.7 0.0 copy-start.8
  0.7 0.0 copy-start.1
  0.7 11.5 %first_tick.3 = (bf16[2048,128]{1,0:T(8,128)(2,1)S(1)}, f32[6,128,128]{2,1,0:T(8,128)S(1)}, f32[16,128]{1,0:T(8,128)S(1)}) custom-call(bf16[1,2,1,4096,128]{4,3,2,1,0:T(8,128)(2,1)} %refs_0_.7, bf16[4096,128]{1,0:T(8,128)(2,1)} %bitcast.6, f32[3,7,1,256]{3,2,1,0:T(1,128)} %bitcast.8, f32[1,256,128]{2,1,0:T(8,128)} %refs_3_.7, f32[32,128]{1,0:T(8,128)} %bitcast.12, ...), custom_call_target="tpu_custom_call" | custom-call | tf_op jit(solution)/shard_map/first_tick/pallas_call | solution.py:339
  12.3 0.0 copy-start.7
  12.3 2.9 %collective-permute-start.1 = (bf16[2048,128]{1,0:T(8,128)(2,1)S(1)}, bf16[2048,128]{1,0:T(8,128)(2,1)S(1)}, u32[]{:S(2)}, u32[]{:S(2)}) collective-permute-start(bf16[2048,128]{1,0:T(8,128)(2,1)S(1)} %get-tuple-element.15), channel_id=1, source_target_pairs={{4,0},{8,4},{12,8},{16,12},{20,16},{24,20},{28,24},{5,1},{9,5},{13... | collective-permute-start | bytes 1572872 | tf_op jit(solution)/shard_map/ppermute | solution.py:24
  15.2 0.0 copy-done.2
  15.2 0.0 copy-done.4
  15.2 0.0 copy-done.5
  15.2 0.0 copy-done.6
  15.2 0.0 copy-done.3
  15.2 0.0 copy-done
  15.3 0.0 copy-done.9
  15.3 0.0 copy-done.8
  15.3 0.0 copy-done.1
  15.3 10.3 %first_tick.2 = (bf16[2048,128]{1,0:T(8,128)(2,1)S(1)}, f32[6,128,128]{2,1,0:T(8,128)S(1)}, f32[16,128]{1,0:T(8,128)S(1)}) custom-call(bf16[1,2,1,4096,128]{4,3,2,1,0:T(8,128)(2,1)S(1)} %copy-done, bf16[4096,128]{1,0:T(8,128)(2,1)S(1)} %bitcast.7, f32[3,7,1,256]{3,2,1,0:T(1,128)S(1)} %bitcast.9, f32[1,256,128]{2,1,0:T(8,128)S(1)} %copy-done.3, ...), custom_call_target="tpu_custom_call" | custom-call | tf_op jit(solution)/shard_map/first_tick/pallas_call | solution.py:339
  25.6 2.6 %collective-permute-start = (bf16[2048,128]{1,0:T(8,128)(2,1)S(1)}, bf16[2048,128]{1,0:T(8,128)(2,1)S(1)}, u32[]{:S(2)}, u32[]{:S(2)}) collective-permute-start(bf16[2048,128]{1,0:T(8,128)(2,1)S(1)} %get-tuple-element.12), channel_id=1, source_target_pairs={{4,0},{8,4},{12,8},{16,12},{20,16},{24,20},{28,24},{5,1},{9,5},{13... | collective-permute-start | bytes 1572872 | tf_op jit(solution)/shard_map/ppermute | solution.py:24
  28.2 0.0 collective-permute-done.1.refs_1_
  28.2 0.0 copy-done.7
  28.2 7.8 %last_tick.2.refs_11_ = bf16[176,128]{1,0:T(8,128)(2,1)S(1)} custom-call(bf16[1,2,1,4096,128]{4,3,2,1,0:T(8,128)(2,1)S(1)} %copy-done, bf16[2048,128]{1,0:T(8,128)(2,1)S(1)} %collective-permute-done.1.refs_1_, f32[3,7,1,256]{3,2,1,0:T(1,128)S(1)} %bitcast.10, f32[1,256,128]{2,1,0:T(8,128)S(1)} %copy-done.3, f32[32,128]{1,0:T(8,128)S(1)} %bitcast.14, ...), custom_call_target="tpu_custom_call" | custom-call | tf_op jit(solution)/shard_map/last_tick/pallas_call | solution.py:339
  36.0 0.0 collective-permute-done.refs_1_
  36.0 7.8 %last_tick.3.refs_0_ = bf16[352,128]{1,0:T(8,128)(2,1)S(1)} custom-call(bf16[1,2,1,4096,128]{4,3,2,1,0:T(8,128)(2,1)S(1)} %copy-done, bf16[2048,128]{1,0:T(8,128)(2,1)S(1)} %collective-permute-done.refs_1_, f32[3,7,1,256]{3,2,1,0:T(1,128)S(1)} %bitcast.11, f32[1,256,128]{2,1,0:T(8,128)S(1)} %copy-done.3, f32[32,128]{1,0:T(8,128)S(1)} %bitcast.15, ...), custom_call_target="tpu_custom_call" | custom-call | tf_op jit(solution)/shard_map/last_tick/pallas_call | solution.py:339
  43.8 3.6 %collective-permute-start.4 = (bf16[352,128]{1,0:T(8,128)(2,1)S(1)}, bf16[352,128]{1,0:T(8,128)(2,1)S(1)}, u32[]{:S(2)}, u32[]{:S(2)}) collective-permute-start(bf16[352,128]{1,0:T(8,128)(2,1)S(1)} %last_tick.3.refs_0_), channel_id=1, source_target_pairs={{0,3},{1,0},{2,1},{3,2},{4,7},{5,4},{6,5},{7,6},{8,11},{9,8},{10,9... | collective-permute-start | bytes 270344 | tf_op jit(solution)/shard_map/ppermute | solution.py:406
  47.4 0.0 collective-permute-start.3
  47.4 1.0 %collective-permute-start.2 = (bf16[352,128]{1,0:T(8,128)(2,1)S(1)}, bf16[352,128]{1,0:T(8,128)(2,1)S(1)}, u32[]{:S(2)}, u32[]{:S(2)}) collective-permute-start(bf16[352,128]{1,0:T(8,128)(2,1)S(1)} %last_tick.3.refs_0_), channel_id=1, source_target_pairs={{0,1},{1,2},{2,3},{3,0},{4,5},{5,6},{6,7},{7,4},{8,9},{9,10},{10,1... | collective-permute-start | bytes 270344 | tf_op jit(solution)/shard_map/ppermute | solution.py:406
  48.4 2.0 %collective-permute-done.4.refs_3_ = bf16[352,128]{1,0:T(8,128)(2,1)S(1)} collective-permute-done((bf16[352,128]{1,0:T(8,128)(2,1)S(1)}, bf16[352,128]{1,0:T(8,128)(2,1)S(1)}, u32[]{:S(2)}, u32[]{:S(2)}) %collective-permute-start.4) | collective-permute-done | bytes 90144 | tf_op jit(solution)/shard_map/ppermute | solution.py:406
  50.5 5.1 %collective-permute-done.3.refs_2_ = bf16[352,128]{1,0:T(8,128)(2,1)S(1)} collective-permute-done((bf16[352,128]{1,0:T(8,128)(2,1)S(1)}, bf16[352,128]{1,0:T(8,128)(2,1)S(1)}, u32[]{:S(2)}, u32[]{:S(2)}) %collective-permute-start.3) | collective-permute-done | bytes 90144 | tf_op jit(solution)/shard_map/ppermute | solution.py:406
  55.6 0.0 collective-permute-done.2.refs_1_
  55.6 0.7 %finish.1 = (f32[3,7,1,256]{3,2,1,0:T(1,128)}, f32[256,128]{1,0:T(8,128)}, f32[32,128]{1,0:T(8,128)}) custom-call(bf16[352,128]{1,0:T(8,128)(2,1)S(1)} %last_tick.3.refs_0_, bf16[352,128]{1,0:T(8,128)(2,1)S(1)} %collective-permute-done.2.refs_1_, bf16[352,128]{1,0:T(8,128)(2,1)S(1)} %collective-permute-done.3.refs_2_, ...), custom_call_target="tpu_custom_call" | custom-call | tf_op jit(solution)/shard_map/finish/pallas_call | solution.py:378
Async XLA Ops:
  0.6 14.6 %copy-start.2 = (bf16[128,768]{1,0:T(8,128)(2,1)S(1)}, bf16[128,768]{1,0:T(8,128)(2,1)}, u32[]{:S(2)}) copy-start(bf16[128,768]{1,0:T(8,128)(2,1)} %constant.12.clone.refs_7_) | copy-start | bytes 589828
  0.6 14.6 %copy-start.4 = (bf16[512,128]{1,0:T(8,128)(2,1)S(1)}, bf16[512,128]{1,0:T(8,128)(2,1)}, u32[]{:S(2)}) copy-start(bf16[512,128]{1,0:T(8,128)(2,1)} %constant.11.clone.refs_6_) | copy-start | bytes 393220
  0.7 14.6 %copy-start.5 = (bf16[256,256]{1,0:T(8,128)(2,1)S(1)}, bf16[256,256]{1,0:T(8,128)(2,1)}, u32[]{:S(2)}) copy-start(bf16[256,256]{1,0:T(8,128)(2,1)} %constant.10.clone.refs_5_) | copy-start | bytes 393220
  0.7 14.6 %copy-start.6 = (bf16[896,128]{1,0:T(8,128)(2,1)S(1)}, bf16[896,128]{1,0:T(8,128)(2,1)}, u32[]{:S(2)}) copy-start(bf16[896,128]{1,0:T(8,128)(2,1)} %constant.13.clone.refs_8_) | copy-start | bytes 688132
  0.7 14.6 %copy-start.3 = (f32[1,256,128]{2,1,0:T(8,128)S(1)}, f32[1,256,128]{2,1,0:T(8,128)}, u32[]{:S(2)}) copy-start(f32[1,256,128]{2,1,0:T(8,128)} %refs_3_.7) | copy-start | bytes 393220
  0.7 14.6 %copy-start = (bf16[1,2,1,4096,128]{4,3,2,1,0:T(8,128)(2,1)S(1)}, bf16[1,2,1,4096,128]{4,3,2,1,0:T(8,128)(2,1)}, u32[]{:S(2)}) copy-start(bf16[1,2,1,4096,128]{4,3,2,1,0:T(8,128)(2,1)} %refs_0_.7) | copy-start | bytes 6291460
  0.7 14.6 %copy-start.9 = (f32[1,4096]{1,0:T(1,128)S(1)}, f32[1,4096]{1,0:T(1,128)}, u32[]{:S(2)}) copy-start(f32[1,4096]{1,0:T(1,128)} %param.14) | copy-start | bytes 49156
  0.7 14.6 %copy-start.8 = (f32[1,3,256,7]{2,0,3,1:T(1,128)S(1)}, f32[1,3,256,7]{2,0,3,1:T(1,128)}, u32[]{:S(2)}) copy-start(f32[1,3,256,7]{2,0,3,1:T(1,128)} %param.12) | copy-start | bytes 64516
  0.7 14.6 %copy-start.1 = (bf16[1,1,4096,128]{3,2,1,0:T(8,128)(2,1)S(1)}, bf16[1,1,4096,128]{3,2,1,0:T(8,128)(2,1)}, u32[]{:S(2)}) copy-start(bf16[1,1,4096,128]{3,2,1,0:T(8,128)(2,1)} %param.11) | copy-start | bytes 3145732
  12.3 16.0 %copy-start.7 = (f32[256,128]{1,0:T(8,128)S(1)}, f32[256,128]{1,0:T(8,128)}, u32[]{:S(2)}) copy-start(f32[256,128]{1,0:T(8,128)} %constant.14.clone.refs_8_) | copy-start | bytes 393220
  12.3 15.9 %collective-permute-start.1 = (bf16[2048,128]{1,0:T(8,128)(2,1)S(1)}, bf16[2048,128]{1,0:T(8,128)(2,1)S(1)}, u32[]{:S(2)}, u32[]{:S(2)}) collective-permute-start(bf16[2048,128]{1,0:T(8,128)(2,1)S(1)} %get-tuple-element.15), channel_id=1, source_target_pairs={{4,0},{8,4},{12,8},{16,12},{20,16},{24,20},{28,24},{5,1},{9,5},{13... | collective-permute-start | bytes 1572872 | tf_op jit(solution)/shard_map/ppermute | solution.py:24
  25.6 10.4 %collective-permute-start = (bf16[2048,128]{1,0:T(8,128)(2,1)S(1)}, bf16[2048,128]{1,0:T(8,128)(2,1)S(1)}, u32[]{:S(2)}, u32[]{:S(2)}) collective-permute-start(bf16[2048,128]{1,0:T(8,128)(2,1)S(1)} %get-tuple-element.12), channel_id=1, source_target_pairs={{4,0},{8,4},{12,8},{16,12},{20,16},{24,20},{28,24},{5,1},{9,5},{13... | collective-permute-start | bytes 1572872 | tf_op jit(solution)/shard_map/ppermute | solution.py:24
  43.8 6.7 %collective-permute-start.4 = (bf16[352,128]{1,0:T(8,128)(2,1)S(1)}, bf16[352,128]{1,0:T(8,128)(2,1)S(1)}, u32[]{:S(2)}, u32[]{:S(2)}) collective-permute-start(bf16[352,128]{1,0:T(8,128)(2,1)S(1)} %last_tick.3.refs_0_), channel_id=1, source_target_pairs={{0,3},{1,0},{2,1},{3,2},{4,7},{5,4},{6,5},{7,6},{8,11},{9,8},{10,9... | collective-permute-start | bytes 270344 | tf_op jit(solution)/shard_map/ppermute | solution.py:406
  47.4 8.1 %collective-permute-start.3 = (bf16[352,128]{1,0:T(8,128)(2,1)S(1)}, bf16[352,128]{1,0:T(8,128)(2,1)S(1)}, u32[]{:S(2)}, u32[]{:S(2)}) collective-permute-start(bf16[352,128]{1,0:T(8,128)(2,1)S(1)} %last_tick.3.refs_0_), channel_id=1, source_target_pairs={{0,2},{1,3},{2,0},{3,1},{4,6},{5,7},{6,4},{7,5},{8,10},{9,11},{10,... | collective-permute-start | bytes 270344 | tf_op jit(solution)/shard_map/ppermute | solution.py:406
  47.4 8.1 %collective-permute-start.2 = (bf16[352,128]{1,0:T(8,128)(2,1)S(1)}, bf16[352,128]{1,0:T(8,128)(2,1)S(1)}, u32[]{:S(2)}, u32[]{:S(2)}) collective-permute-start(bf16[352,128]{1,0:T(8,128)(2,1)S(1)} %last_tick.3.refs_0_), channel_id=1, source_target_pairs={{0,1},{1,2},{2,3},{3,0},{4,5},{5,6},{6,7},{7,4},{8,9},{9,10},{10,1... | collective-permute-start | bytes 270344 | tf_op jit(solution)/shard_map/ppermute | solution.py:406

commit v4 on v3

--- a/solution.py
+++ b/solution.py
@@ -46,7 +46,7 @@
     unshift = np.concatenate([np.eye(length, k=-lag) for lag in range(taps)], axis=0)
     return (
         np.concatenate(split(forward), axis=0),
-        np.concatenate(split(inverse), axis=0),
+        np.concatenate(split(inverse), axis=1),
         inverse.astype(np.float32),
         shift.astype(jnp.bfloat16),
         unshift.astype(jnp.bfloat16),
@@ -97,7 +97,7 @@
 
     def setup(self):
         first = lax.broadcasted_iota(jnp.int32, (1, LANES), 1) == 0
-        h = self.med[0].astype(BF16)
+        h = self.med[...].astype(BF16)
         hh = mm(jnp.concatenate([h, h], axis=1), self.fwd[...])
         hr, hi = hh[:, :LANES], hh[:, LANES:]
         self.coef[0] = hr
@@ -114,7 +114,7 @@
 
     def start(self, block, slot):
         taps_at, skip_at, xs = self.taps_at[slot], self.skip_at[slot], self.xs[slot]
-        x = self.x[0, 0, 0, pl.ds(self.rows(block), SUB), :]
+        x = self.x[pl.ds(self.rows(block), SUB), :]
         xs[:, LANES:] = mm(x, self.shift[...])
         xs[:, :LANES] = x.astype(F32)
         mine = self.columns[self.groups(block), :]
@@ -166,8 +166,8 @@
             spec[rg, LANES:] = (gi * cc - gr * cb).astype(BF16)
             for i, value in enumerate((pr * gr, pi * gi, pr * gi - pi * gr)):
                 terms[i, 8 * k : 8 * k + 8, :] = value[:8] + value[8:]
-        both = spec[...]
-        self.res[slot][...] = mm(jnp.concatenate([both, both], axis=1), self.inv[...])
+        wide = mm(spec[...], self.inv[...])
+        self.res[slot][...] = wide[:, :LANES] + wide[:, LANES:]
 
     def gradients(self, block, slot):
         taps_at, skip_at, xs, feat, res, sums, hats, corr = (
@@ -187,7 +187,8 @@
             sums[r] = (gm * product).astype(BF16)
             gfb = jnp.concatenate([g.astype(BF16) for g in gf], axis=0)
             xsb = jnp.concatenate(
-                [xs[r, LANES * j : LANES * (j + 1)].astype(BF16) for j in range(self.taps)]
+                [self.x[pl.ds(self.rows(block) + GROUP * k, GROUP), :]]
+                + [xs[r, LANES * j : LANES * (j + 1)].astype(BF16) for j in range(1, self.taps)]
                 + [jnp.zeros((GROUP, LANES), BF16)] * (LANES // GROUP - self.taps),
                 axis=0,
             )
@@ -228,22 +229,29 @@
             self.features(t, t % RING)
         self.filter(0)
 
+        order = "aecbd" if self.last else "cadbe"
+
+        def step(t, u, left):
+            stages = {
+                "a": (3, self.start, t + 3, (u + 3) % RING),
+                "b": (2, self.features, t + 2, (u + 2) % RING),
+                "c": (1, self.filter, (u + 1) % RING),
+                "d": (0, self.gradients, t, u),
+                "e": (0, self.finish, jnp.maximum(t - 1, 0), (u - 1) % RING),
+            }
+            for name in order:
+                ahead, stage, *where = stages[name]
+                if ahead < left:
+                    stage(*where)
+
         def turn(index, _):
             for u in range(RING):
-                t = RING * index + u
-                stages = {
-                    "a": (self.start, jnp.minimum(t + 3, blocks - 1), (u + 3) % RING),
-                    "b": (self.features, jnp.minimum(t + 2, blocks - 1), (u + 2) % RING),
-                    "c": (self.filter, (u + 1) % RING),
-                    "d": (self.gradients, t, u),
-                    "e": (self.finish, jnp.maximum(t - 1, 0), (u - 1) % RING),
-                }
-                for name in "aecbd" if self.last else "cadbe":
-                    stage, *where = stages[name]
-                    stage(*where)
+                step(RING * index + u, u, RING)
             return 0
 
-        lax.fori_loop(0, blocks // RING, turn, 0)
+        lax.fori_loop(0, blocks // RING - 1, turn, 0)
+        for u in range(RING):
+            step(blocks - RING + u, u, RING - u)
         self.finish(blocks - 1, (blocks - 1) % RING)
 
     def message(self):
@@ -267,14 +275,26 @@
         self.msg[at : at + mine.shape[0]] = mine
 
 
-def tick_kernel(last, taps, counts, *refs):
+def tick_kernel(last, taps, counts, where, *refs):
     ins, outs, scratch = refs[: counts[0]], refs[counts[0] : sum(counts)], refs[sum(counts) :]
-    tick = Tick(last, taps, ins, outs, scratch)
-    blocks = tick.x.shape[-2] // SUB
-    tick.setup()
-    tick.run(blocks)
+    x, cot, f, med, skip = ins[:5]
+    tick, chunk, at, channels = where
+    if chunk is None:
+        views = (x.at[0, 0, 0], cot, f, med.at[0], skip)
+    else:
+        groups, rows = channels // GROUP, channels // LANES
+        views = (
+            x.at[0, tick, 0, pl.ds(chunk * channels, channels), :],
+            cot.at[pl.ds(at * channels, channels), :],
+            f.at[:, :, :, pl.ds(chunk * groups, groups)],
+            med.at[0, pl.ds(chunk * groups, groups), :],
+            skip.at[pl.ds(chunk * rows, rows), :],
+        )
+    work = Tick(last, taps, (*views, *ins[5:]), outs, scratch)
+    work.setup()
+    work.run(channels // SUB)
     if last:
-        tick.message()
+        work.message()
 
 
 def in_hbm(array):
@@ -293,7 +313,8 @@
     at = chunk if cot.shape[0] == total else 0
     ins = [saved, cot, filters, medium, skip_rows, forward, inverse, shift]
     ins += [inverse_full] if last else [unshift]
-    if not last and chunk == 0:
+    fetch = not last and chunk == 0
+    if fetch:
         ins = [in_hbm(jnp.asarray(a)) for a in ins]
     ins += [*prior] if last else []
     in_specs = [
@@ -303,6 +324,9 @@
         pl.BlockSpec((1, groups, length), lambda i: (0, chunk, 0)),
         pl.BlockSpec((channels // LANES, LANES), lambda i: (chunk, 0)),
     ] + [full(a) for a in ins[5:]]
+    whole = pl.BlockSpec(memory_space=pltpu.VMEM)
+    if not fetch:
+        in_specs = [whole] * len(ins)
     acc_shape = (6, groups, LANES)
     skip_shape = (channels // LANES, LANES)
     ring = [
@@ -337,11 +361,14 @@
             jax.ShapeDtypeStruct(skip_shape, F32),
         ]
     return pl.pallas_call(
-        functools.partial(tick_kernel, last, taps, (len(ins), len(outs))),
+        functools.partial(
+            tick_kernel, last, taps, (len(ins), len(outs)),
+            (tick, None if fetch else chunk, at, channels),
+        ),
         out_shape=outs,
         grid=(1,),
         in_specs=in_specs,
-        out_specs=[full(a) for a in outs],
+        out_specs=[whole] * len(outs),
         scratch_shapes=scratch,
         compiler_params=pltpu.CompilerParams(vmem_limit_bytes=48 << 20),
         name="last_tick" if last else "first_tick",
@@ -402,10 +429,11 @@
     message = []
     for c in range(chunks):
         message = run_tick(saved, incoming[c], *rest, 1, c, chunks, (*prior[c], *message))
-    parts = [*message] + [
-        lax.ppermute(message[0], "replica", [(i, (i + by) % replicas) for i in range(replicas)])
-        for by in range(1, replicas)
-    ]
+    even = replicas & (replicas - 1) == 0
+    parts = [*message]
+    for by in range(1, replicas):
+        pairs = [(i, i ^ by if even else (i + by) % replicas) for i in range(replicas)]
+        parts.append(lax.ppermute(message[0], "replica", pairs))
     short, medium, skip_grad = finish(parts, groups, channels, taps, chunks)
     return (
         jnp.transpose(short, (2, 0, 3, 1)),

time: 57.4 us -> 53.3 us (0.929); the launches traced: 56.3 us -> 52.9 us
  Pallas kernels: 38.1 us -> 35.1 us
    pallas_call x4, Pallas kernels: 37.4 us -> 34.4 us  [run_tick(): pl.pallas_call(functools.partial(tick_kernel, last, taps, (len(ins), len(...]
  transfers between devices with their start and end apart: 5 -> 5, of which waited for: 2 -> 2; matrix products, arithmetic and copies ran while one was open for 0% -> 0% of each run, Pallas kernels for 32% -> 31%
where the time goes in v4:
time: 53.3 us; the launch traced here: 52.9 us
  Pallas kernels  35.1 us (66%)
  starting transfers between devices  10.1 us (19%)
  waiting for transfers between devices  6.79 us (13%)
  between operations  0.83 us (2%)
    pallas_call x4, Pallas kernels, run_tick(): pl.pallas_call(functools.partial(tick_kernel, last, taps, (len(ins), len(...  34.4 us
    ppermute x3, waiting for transfers between devices, body(): parts.append(lax.ppermute(message[0], 'replica', pairs))  6.78 us
    ppermute x2, starting transfers between devices, shifted(): return lax.ppermute(array, axis, pairs)  5.67 us
    ppermute x3, starting transfers between devices, body(): parts.append(lax.ppermute(message[0], 'replica', pairs))  4.42 us
  transfers between devices with their start and end apart: 5, of which 2 were waited for; matrix products, arithmetic and copies ran while one was open for 0% of the time, Pallas kernels for 31%

profile of v4, /device:TPU:4, one launch (start us, length us, event | category | flops | bytes accessed | tf_op | source)
XLA Modules:
  0.0 52.9 jit_solution(2935639611751917731)
XLA Ops:
  0.6 0.0 copy-start.2
  0.6 0.0 copy-start.4
  0.7 0.0 copy-start.5
  0.7 0.0 copy-start.6
  0.7 0.0 copy-start.3
  0.7 0.0 copy-start
  0.7 0.0 copy-start.9
  0.7 0.0 copy-start.8
  0.7 0.0 copy-start.1
  0.7 10.3 %first_tick.3 = (bf16[2048,128]{1,0:T(8,128)(2,1)S(1)}, f32[6,128,128]{2,1,0:T(8,128)S(1)}, f32[16,128]{1,0:T(8,128)S(1)}) custom-call(bf16[1,2,1,4096,128]{4,3,2,1,0:T(8,128)(2,1)} %refs_0_.7, bf16[4096,128]{1,0:T(8,128)(2,1)} %bitcast.6, f32[3,7,1,256]{3,2,1,0:T(1,128)} %bitcast.8, f32[1,256,128]{2,1,0:T(8,128)} %refs_3_.7, f32[32,128]{1,0:T(8,128)} %bitcast.12, ...), custom_call_target="tpu_custom_call" | custom-call | tf_op jit(solution)/shard_map/first_tick/pallas_call | solution.py:363
  11.0 0.0 copy-start.7
  11.0 2.9 %collective-permute-start.1 = (bf16[2048,128]{1,0:T(8,128)(2,1)S(1)}, bf16[2048,128]{1,0:T(8,128)(2,1)S(1)}, u32[]{:S(2)}, u32[]{:S(2)}) collective-permute-start(bf16[2048,128]{1,0:T(8,128)(2,1)S(1)} %get-tuple-element.15), channel_id=1, source_target_pairs={{4,0},{8,4},{12,8},{16,12},{20,16},{24,20},{28,24},{5,1},{9,5},{13... | collective-permute-start | bytes 1572872 | tf_op jit(solution)/shard_map/ppermute | solution.py:24
  13.9 0.0 copy-done.2
  13.9 0.0 copy-done.4
  13.9 0.0 copy-done.5
  14.0 0.0 copy-done.6
  14.0 0.0 copy-done.3
  14.0 0.0 copy-done
  14.0 0.0 copy-done.9
  14.0 0.0 copy-done.8
  14.0 0.0 copy-done.1
  14.0 9.0 %first_tick.2 = (bf16[2048,128]{1,0:T(8,128)(2,1)S(1)}, f32[6,128,128]{2,1,0:T(8,128)S(1)}, f32[16,128]{1,0:T(8,128)S(1)}) custom-call(bf16[1,2,1,4096,128]{4,3,2,1,0:T(8,128)(2,1)S(1)} %copy-done, bf16[4096,128]{1,0:T(8,128)(2,1)S(1)} %bitcast.7, f32[3,7,1,256]{3,2,1,0:T(1,128)S(1)} %bitcast.9, f32[1,256,128]{2,1,0:T(8,128)S(1)} %copy-done.3, ...), custom_call_target="tpu_custom_call" | custom-call | tf_op jit(solution)/shard_map/first_tick/pallas_call | solution.py:363
  23.0 2.8 %collective-permute-start = (bf16[2048,128]{1,0:T(8,128)(2,1)S(1)}, bf16[2048,128]{1,0:T(8,128)(2,1)S(1)}, u32[]{:S(2)}, u32[]{:S(2)}) collective-permute-start(bf16[2048,128]{1,0:T(8,128)(2,1)S(1)} %get-tuple-element.12), channel_id=1, source_target_pairs={{4,0},{8,4},{12,8},{16,12},{20,16},{24,20},{28,24},{5,1},{9,5},{13... | collective-permute-start | bytes 1572872 | tf_op jit(solution)/shard_map/ppermute | solution.py:24
  25.8 0.0 collective-permute-done.1.refs_1_
  25.8 0.0 copy-done.7
  25.8 7.5 %last_tick.2.refs_11_ = bf16[176,128]{1,0:T(8,128)(2,1)S(1)} custom-call(bf16[1,2,1,4096,128]{4,3,2,1,0:T(8,128)(2,1)S(1)} %copy-done, bf16[2048,128]{1,0:T(8,128)(2,1)S(1)} %collective-permute-done.1.refs_1_, f32[3,7,1,256]{3,2,1,0:T(1,128)S(1)} %bitcast.10, f32[1,256,128]{2,1,0:T(8,128)S(1)} %copy-done.3, f32[32,128]{1,0:T(8,128)S(1)} %bitcast.14, ...), custom_call_target="tpu_custom_call" | custom-call | tf_op jit(solution)/shard_map/last_tick/pallas_call | solution.py:363
  33.4 0.0 collective-permute-done.refs_1_
  33.4 7.6 %last_tick.3.refs_0_ = bf16[352,128]{1,0:T(8,128)(2,1)S(1)} custom-call(bf16[1,2,1,4096,128]{4,3,2,1,0:T(8,128)(2,1)S(1)} %copy-done, bf16[2048,128]{1,0:T(8,128)(2,1)S(1)} %collective-permute-done.refs_1_, f32[3,7,1,256]{3,2,1,0:T(1,128)S(1)} %bitcast.11, f32[1,256,128]{2,1,0:T(8,128)S(1)} %copy-done.3, f32[32,128]{1,0:T(8,128)S(1)} %bitcast.15, ...), custom_call_target="tpu_custom_call" | custom-call | tf_op jit(solution)/shard_map/last_tick/pallas_call | solution.py:363
  41.0 3.6 %collective-permute-start.4 = (bf16[352,128]{1,0:T(8,128)(2,1)S(1)}, bf16[352,128]{1,0:T(8,128)(2,1)S(1)}, u32[]{:S(2)}, u32[]{:S(2)}) collective-permute-start(bf16[352,128]{1,0:T(8,128)(2,1)S(1)} %last_tick.3.refs_0_), channel_id=1, source_target_pairs={{0,3},{1,2},{2,1},{3,0},{4,7},{5,6},{6,5},{7,4},{8,11},{9,10},{10,... | collective-permute-start | bytes 270344 | tf_op jit(solution)/shard_map/ppermute | solution.py:436
  44.6 0.0 collective-permute-start.3
  44.6 0.8 %collective-permute-start.2 = (bf16[352,128]{1,0:T(8,128)(2,1)S(1)}, bf16[352,128]{1,0:T(8,128)(2,1)S(1)}, u32[]{:S(2)}, u32[]{:S(2)}) collective-permute-start(bf16[352,128]{1,0:T(8,128)(2,1)S(1)} %last_tick.3.refs_0_), channel_id=1, source_target_pairs={{0,1},{1,0},{2,3},{3,2},{4,5},{5,4},{6,7},{7,6},{8,9},{9,8},{10,11... | collective-permute-start | bytes 270344 | tf_op jit(solution)/shard_map/ppermute | solution.py:436
  45.4 2.7 %collective-permute-done.4.refs_3_ = bf16[352,128]{1,0:T(8,128)(2,1)S(1)} collective-permute-done((bf16[352,128]{1,0:T(8,128)(2,1)S(1)}, bf16[352,128]{1,0:T(8,128)(2,1)S(1)}, u32[]{:S(2)}, u32[]{:S(2)}) %collective-permute-start.4) | collective-permute-done | bytes 90144 | tf_op jit(solution)/shard_map/ppermute | solution.py:436
  48.1 4.1 %collective-permute-done.3.refs_2_ = bf16[352,128]{1,0:T(8,128)(2,1)S(1)} collective-permute-done((bf16[352,128]{1,0:T(8,128)(2,1)S(1)}, bf16[352,128]{1,0:T(8,128)(2,1)S(1)}, u32[]{:S(2)}, u32[]{:S(2)}) %collective-permute-start.3) | collective-permute-done | bytes 90144 | tf_op jit(solution)/shard_map/ppermute | solution.py:436
  52.2 0.0 collective-permute-done.2.refs_1_
  52.2 0.7 %finish.1 = (f32[3,7,1,256]{3,2,1,0:T(1,128)}, f32[256,128]{1,0:T(8,128)}, f32[32,128]{1,0:T(8,128)}) custom-call(bf16[352,128]{1,0:T(8,128)(2,1)S(1)} %last_tick.3.refs_0_, bf16[352,128]{1,0:T(8,128)(2,1)S(1)} %collective-permute-done.2.refs_1_, bf16[352,128]{1,0:T(8,128)(2,1)S(1)} %collective-permute-done.3.refs_2_, ...), custom_call_target="tpu_custom_call" | custom-call | tf_op jit(solution)/shard_map/finish/pallas_call | solution.py:405
Async XLA Ops:
  0.6 13.3 %copy-start.2 = (bf16[128,768]{1,0:T(8,128)(2,1)S(1)}, bf16[128,768]{1,0:T(8,128)(2,1)}, u32[]{:S(2)}) copy-start(bf16[128,768]{1,0:T(8,128)(2,1)} %constant.12.clone.refs_7_) | copy-start | bytes 589828
  0.6 13.3 %copy-start.4 = (bf16[256,256]{1,0:T(8,128)(2,1)S(1)}, bf16[256,256]{1,0:T(8,128)(2,1)}, u32[]{:S(2)}) copy-start(bf16[256,256]{1,0:T(8,128)(2,1)} %constant.11.clone.refs_6_) | copy-start | bytes 393220
  0.7 13.3 %copy-start.5 = (bf16[256,256]{1,0:T(8,128)(2,1)S(1)}, bf16[256,256]{1,0:T(8,128)(2,1)}, u32[]{:S(2)}) copy-start(bf16[256,256]{1,0:T(8,128)(2,1)} %constant.10.clone.refs_5_) | copy-start | bytes 393220
  0.7 13.3 %copy-start.6 = (bf16[896,128]{1,0:T(8,128)(2,1)S(1)}, bf16[896,128]{1,0:T(8,128)(2,1)}, u32[]{:S(2)}) copy-start(bf16[896,128]{1,0:T(8,128)(2,1)} %constant.13.clone.refs_8_) | copy-start | bytes 688132
  0.7 13.3 %copy-start.3 = (f32[1,256,128]{2,1,0:T(8,128)S(1)}, f32[1,256,128]{2,1,0:T(8,128)}, u32[]{:S(2)}) copy-start(f32[1,256,128]{2,1,0:T(8,128)} %refs_3_.7) | copy-start | bytes 393220
  0.7 13.3 %copy-start = (bf16[1,2,1,4096,128]{4,3,2,1,0:T(8,128)(2,1)S(1)}, bf16[1,2,1,4096,128]{4,3,2,1,0:T(8,128)(2,1)}, u32[]{:S(2)}) copy-start(bf16[1,2,1,4096,128]{4,3,2,1,0:T(8,128)(2,1)} %refs_0_.7) | copy-start | bytes 6291460
  0.7 13.3 %copy-start.9 = (f32[1,4096]{1,0:T(1,128)S(1)}, f32[1,4096]{1,0:T(1,128)}, u32[]{:S(2)}) copy-start(f32[1,4096]{1,0:T(1,128)} %param.14) | copy-start | bytes 49156
  0.7 13.3 %copy-start.8 = (f32[1,3,256,7]{2,0,3,1:T(1,128)S(1)}, f32[1,3,256,7]{2,0,3,1:T(1,128)}, u32[]{:S(2)}) copy-start(f32[1,3,256,7]{2,0,3,1:T(1,128)} %param.12) | copy-start | bytes 64516
  0.7 13.3 %copy-start.1 = (bf16[1,1,4096,128]{3,2,1,0:T(8,128)(2,1)S(1)}, bf16[1,1,4096,128]{3,2,1,0:T(8,128)(2,1)}, u32[]{:S(2)}) copy-start(bf16[1,1,4096,128]{3,2,1,0:T(8,128)(2,1)} %param.11) | copy-start | bytes 3145732
  11.0 14.8 %copy-start.7 = (f32[256,128]{1,0:T(8,128)S(1)}, f32[256,128]{1,0:T(8,128)}, u32[]{:S(2)}) copy-start(f32[256,128]{1,0:T(8,128)} %constant.14.clone.refs_8_) | copy-start | bytes 393220
  11.0 14.8 %collective-permute-start.1 = (bf16[2048,128]{1,0:T(8,128)(2,1)S(1)}, bf16[2048,128]{1,0:T(8,128)(2,1)S(1)}, u32[]{:S(2)}, u32[]{:S(2)}) collective-permute-start(bf16[2048,128]{1,0:T(8,128)(2,1)S(1)} %get-tuple-element.15), channel_id=1, source_target_pairs={{4,0},{8,4},{12,8},{16,12},{20,16},{24,20},{28,24},{5,1},{9,5},{13... | collective-permute-start | bytes 1572872 | tf_op jit(solution)/shard_map/ppermute | solution.py:24
  23.0 10.3 %collective-permute-start = (bf16[2048,128]{1,0:T(8,128)(2,1)S(1)}, bf16[2048,128]{1,0:T(8,128)(2,1)S(1)}, u32[]{:S(2)}, u32[]{:S(2)}) collective-permute-start(bf16[2048,128]{1,0:T(8,128)(2,1)S(1)} %get-tuple-element.12), channel_id=1, source_target_pairs={{4,0},{8,4},{12,8},{16,12},{20,16},{24,20},{28,24},{5,1},{9,5},{13... | collective-permute-start | bytes 1572872 | tf_op jit(solution)/shard_map/ppermute | solution.py:24
  41.0 7.1 %collective-permute-start.4 = (bf16[352,128]{1,0:T(8,128)(2,1)S(1)}, bf16[352,128]{1,0:T(8,128)(2,1)S(1)}, u32[]{:S(2)}, u32[]{:S(2)}) collective-permute-start(bf16[352,128]{1,0:T(8,128)(2,1)S(1)} %last_tick.3.refs_0_), channel_id=1, source_target_pairs={{0,3},{1,2},{2,1},{3,0},{4,7},{5,6},{6,5},{7,4},{8,11},{9,10},{10,... | collective-permute-start | bytes 270344 | tf_op jit(solution)/shard_map/ppermute | solution.py:436
  44.6 7.6 %collective-permute-start.3 = (bf16[352,128]{1,0:T(8,128)(2,1)S(1)}, bf16[352,128]{1,0:T(8,128)(2,1)S(1)}, u32[]{:S(2)}, u32[]{:S(2)}) collective-permute-start(bf16[352,128]{1,0:T(8,128)(2,1)S(1)} %last_tick.3.refs_0_), channel_id=1, source_target_pairs={{0,2},{1,3},{2,0},{3,1},{4,6},{5,7},{6,4},{7,5},{8,10},{9,11},{10,... | collective-permute-start | bytes 270344 | tf_op jit(solution)/shard_map/ppermute | solution.py:436
  44.6 7.6 %collective-permute-start.2 = (bf16[352,128]{1,0:T(8,128)(2,1)S(1)}, bf16[352,128]{1,0:T(8,128)(2,1)S(1)}, u32[]{:S(2)}, u32[]{:S(2)}) collective-permute-start(bf16[352,128]{1,0:T(8,128)(2,1)S(1)} %last_tick.3.refs_0_), channel_id=1, source_target_pairs={{0,1},{1,0},{2,3},{3,2},{4,5},{5,4},{6,7},{7,6},{8,9},{9,8},{10,11... | collective-permute-start | bytes 270344 | tf_op jit(solution)/shard_map/ppermute | solution.py:436

commit v5 on v4

--- a/solution.py
+++ b/solution.py
@@ -15,7 +15,6 @@
 
 F32 = jnp.float32
 BF16 = jnp.bfloat16
-PRECISE = lax.Precision.HIGHEST
 
 
 def shifted(array, axis, by):
@@ -43,24 +42,26 @@
     weight[0] = weight[length] = 1.0 / points
     inverse = weight * forward.T
     shift = np.concatenate([np.eye(length, k=lag) for lag in range(1, taps)], axis=1)
-    unshift = np.concatenate([np.eye(length, k=-lag) for lag in range(taps)], axis=0)
+    unshift = np.concatenate([np.eye(length, k=-lag) for lag in range(1, taps)], axis=0)
     return (
         np.concatenate(split(forward), axis=0),
         np.concatenate(split(inverse), axis=1),
-        inverse.astype(np.float32),
         shift.astype(jnp.bfloat16),
         unshift.astype(jnp.bfloat16),
     )
 
 
-def nt(left, right, precision=None):
-    return lax.dot_general(
-        left, right, (((1,), (1,)), ((), ())), precision=precision, preferred_element_type=F32
-    )
-
-
-def mm(left, right, precision=None):
-    return jnp.dot(left, right, precision=precision, preferred_element_type=F32)
+def nt(left, right):
+    return lax.dot_general(left, right, (((1,), (1,)), ((), ())), preferred_element_type=F32)
+
+
+def mm(left, right):
+    return jnp.dot(left, right, preferred_element_type=F32)
+
+
+def halves(value):
+    high = value.astype(BF16)
+    return high, (value - high.astype(F32)).astype(BF16)
 
 
 def row(ref, *index):
@@ -78,16 +79,17 @@
         (self.x, self.cot, self.f, self.med, self.skip, self.fwd, self.inv, self.shift) = ins[:8]
         scratch = list(scratch)
         if last:
-            self.finv, self.acc_in, self.skip_in, *self.earlier = ins[8:]
+            self.acc_in, self.skip_in, self.coef, self.columns = ins[8:12]
+            self.earlier = ins[12:]
             (self.msg,) = outs
             self.acc, self.skips = scratch.pop(0), scratch.pop(0)
         else:
             (self.unshift,) = ins[8:]
-            self.gin, self.acc, self.skips = outs
-        self.columns, self.coef, self.turn = scratch[:3]
-        rings = [scratch[i : i + RING] for i in range(3, len(scratch), RING)]
+            self.gin, self.acc, self.skips, self.coef, self.columns = outs
+            self.turn = scratch.pop(0)
+        rings = [scratch[i : i + RING] for i in range(0, len(scratch), RING)]
         (self.taps_at, self.coef_at, self.skip_at, self.xs, self.feat, self.lows, self.hat,
-         self.spec, self.res, self.terms, self.sums, self.hats, self.corr) = rings
+         self.spec, self.res, self.terms, self.sums, self.hats, self.corr, self.base) = rings
 
     def rows(self, block):
         return pl.multiple_of(block * SUB, SUB)
@@ -199,7 +201,10 @@
                     for m in range(3):
                         tap = row(taps_at, m * self.taps + j, slice(k, k + 1))
                         total = tap * gf[m] if total is None else total + tap * gf[m]
-                    hats[r, LANES * j : LANES * (j + 1)] = total.astype(BF16)
+                    if j == 0:
+                        self.base[slot][r] = cot + total
+                    else:
+                        hats[r, LANES * (j - 1) : LANES * j] = total.astype(BF16)
 
     def finish(self, block, slot):
         terms, corr = self.terms[slot], self.corr[slot]
@@ -215,7 +220,7 @@
             self.acc[i, self.groups(block), :] = total
         if not self.last:
             rows = pl.ds(self.rows(block), SUB)
-            gin = mm(self.hats[slot][...], self.unshift[...]) + self.cot[rows, :].astype(F32)
+            gin = mm(self.hats[slot][...], self.unshift[...]) + self.base[slot][...]
             self.gin[rows, :] = gin.astype(BF16)
         sums = nt(jnp.ones((8, LANES), BF16), self.sums[slot][...])
         for q in range(SUB // LANES):
@@ -229,7 +234,7 @@
             self.features(t, t % RING)
         self.filter(0)
 
-        order = "aecbd" if self.last else "cadbe"
+        order = "cabde" if self.last else "acdbe"
 
         def step(t, u, left):
             stages = {
@@ -259,13 +264,18 @@
         total = [self.acc[i] + self.acc_in[i] for i in range(6)]
         real = total[0] + jnp.where(first, 0.0, total[1])
         imag = jnp.where(first, total[1], total[2])
-        both = jnp.concatenate([real, imag], axis=1)
+        high, low = halves(jnp.concatenate([real, imag], axis=1))
+        inv = self.inv[...]
+        wide = mm(high, inv)
+        medium = wide[:, :LANES] + (wide[:, LANES:] + mm(low, inv[:, :LANES]))
         pick = (
             lax.broadcasted_iota(jnp.int32, (8, LANES), 1) // GROUP
             == lax.broadcasted_iota(jnp.int32, (8, LANES), 0)
-        ).astype(F32)
-        pieces = [mm(both, self.finv[...], PRECISE), self.skips[...] + self.skip_in[...]]
-        pieces += [nt(pick, total[3 + m], PRECISE) for m in range(3)]
+        ).astype(BF16)
+        pieces = [medium, self.skips[...] + self.skip_in[...]]
+        for m in range(3):
+            high, low = halves(total[3 + m])
+            pieces.append(nt(pick, high) + nt(pick, low))
         pieces.append(jnp.zeros((8, LANES), F32))
         mine = jnp.concatenate(pieces, axis=0).astype(BF16)
         at = 0
@@ -291,7 +301,8 @@
             skip.at[pl.ds(chunk * rows, rows), :],
         )
     work = Tick(last, taps, (*views, *ins[5:]), outs, scratch)
-    work.setup()
+    if not last:
+        work.setup()
     work.run(channels // SUB)
     if last:
         work.message()
@@ -307,12 +318,12 @@
     channels = total // chunks
     taps = filters.shape[1]
     groups = channels // GROUP
-    forward, inverse, inverse_full, shift, unshift = tables(length, taps)
+    forward, inverse, shift, unshift = tables(length, taps)
     ng = SUB // GROUP
     full = lambda a: pl.BlockSpec(a.shape, lambda i: (0,) * len(a.shape))
     at = chunk if cot.shape[0] == total else 0
     ins = [saved, cot, filters, medium, skip_rows, forward, inverse, shift]
-    ins += [inverse_full] if last else [unshift]
+    ins += [] if last else [unshift]
     fetch = not last and chunk == 0
     if fetch:
         ins = [in_hbm(jnp.asarray(a)) for a in ins]
@@ -341,15 +352,14 @@
         pltpu.VMEM((2 * SUB, LANES), F32),
         pltpu.VMEM((6, 8 * ng, LANES), F32),
         pltpu.VMEM((SUB, LANES), BF16),
-        pltpu.VMEM((SUB, taps * LANES), BF16),
+        pltpu.VMEM((SUB, (taps - 1) * LANES), BF16),
         pltpu.VMEM((ng, 3 * GROUP, LANES), F32),
+        pltpu.VMEM((SUB, LANES), F32),
     ]
-    scratch = [pltpu.VMEM(acc_shape, F32), pltpu.VMEM(skip_shape, F32)] if last else []
-    scratch += [
-        pltpu.VMEM((groups, LANES), F32),
-        pltpu.VMEM((3, groups, LANES), F32),
-        pltpu.VMEM((LANES, LANES), F32),
-    ]
+    if last:
+        scratch = [pltpu.VMEM(acc_shape, F32), pltpu.VMEM(skip_shape, F32)]
+    else:
+        scratch = [pltpu.VMEM((LANES, LANES), F32)]
     scratch += [ref for ref in ring for _ in range(RING)]
     if last:
         rows = (groups + channels // LANES + 32) * (chunk + 1)
@@ -359,6 +369,8 @@
             jax.ShapeDtypeStruct((channels, length), BF16),
             jax.ShapeDtypeStruct(acc_shape, F32),
             jax.ShapeDtypeStruct(skip_shape, F32),
+            jax.ShapeDtypeStruct((3, groups, LANES), F32),
+            jax.ShapeDtypeStruct((groups, LANES), F32),
         ]
     return pl.pallas_call(
         functools.partial(

time: 53.3 us -> 51.2 us (0.961)
  Pallas kernels: 35.1 us -> 32.6 us
  waiting for transfers between devices: 6.79 us -> 7.63 us
    pallas_call x4, Pallas kernels: 34.4 us -> 31.9 us  [run_tick(): pl.pallas_call(functools.partial(tick_kernel, last, taps, (len(ins), len(...]
    ppermute x3, waiting for transfers between devices: 6.78 us -> 7.62 us  [body(): parts.append(lax.ppermute(message[0], 'replica', pairs))]
  transfers between devices with their start and end apart: 5 -> 5, of which waited for: 2 -> 2; matrix products, arithmetic and copies ran while one was open for 0% -> 0% of each run, Pallas kernels for 31% -> 30%
where the time goes in v5:
time: 51.2 us; the launch traced here: 51 us
  Pallas kernels  32.6 us (64%)
  starting transfers between devices  9.95 us (19%)
  waiting for transfers between devices  7.63 us (15%)
  between operations  0.8 us (2%)
    pallas_call x4, Pallas kernels, run_tick(): pl.pallas_call(functools.partial(tick_kernel, last, taps, (len(ins), len(...  31.9 us
    ppermute x3, waiting for transfers between devices, body(): parts.append(lax.ppermute(message[0], 'replica', pairs))  7.62 us
    ppermute x2, starting transfers between devices, shifted(): return lax.ppermute(array, axis, pairs)  5.55 us
    ppermute x3, starting transfers between devices, body(): parts.append(lax.ppermute(message[0], 'replica', pairs))  4.4 us
  transfers between devices with their start and end apart: 5, of which 2 were waited for; matrix products, arithmetic and copies ran while one was open for 0% of the time, Pallas kernels for 30%

profile of v5, /device:TPU:4, one launch (start us, length us, event | category | flops | bytes accessed | tf_op | source)
XLA Modules:
  0.0 51.0 jit_solution(17212015645184402713)
XLA Ops:
  0.6 0.0 copy-start.2
  0.6 0.0 copy-start.4
  0.7 0.0 copy-start.5
  0.7 0.0 copy-start.6
  0.7 0.0 copy-start.3
  0.7 0.0 copy-start
  0.7 0.0 copy-start.8
  0.7 0.0 copy-start.7
  0.7 0.0 copy-start.1
  0.7 9.9 %first_tick.3 = (bf16[2048,128]{1,0:T(8,128)(2,1)S(1)}, f32[6,128,128]{2,1,0:T(8,128)S(1)}, f32[16,128]{1,0:T(8,128)S(1)}, f32[3,128,128]{2,1,0:T(8,128)S(1)}, f32[128,128]{1,0:T(8,128)S(1)}) custom-call(bf16[1,2,1,4096,128]{4,3,2,1,0:T(8,128)(2,1)} %refs_0_.7, bf16[4096,128]{1,0:T(8,128)(2,1)} %bitcast.6, f32[3,7,1,256]{3,2,1,0:T(1,128)} %bitcast.8, ...), custom_call_target="tpu_custom_call" | custom-call | tf_op jit(solution)/shard_map/first_tick/pallas_call | solution.py:375
  10.7 2.8 %collective-permute-start.1 = (bf16[2048,128]{1,0:T(8,128)(2,1)S(1)}, bf16[2048,128]{1,0:T(8,128)(2,1)S(1)}, u32[]{:S(2)}, u32[]{:S(2)}) collective-permute-start(bf16[2048,128]{1,0:T(8,128)(2,1)S(1)} %get-tuple-element.21), channel_id=1, source_target_pairs={{4,0},{8,4},{12,8},{16,12},{20,16},{24,20},{28,24},{5,1},{9,5},{13... | collective-permute-start | bytes 1572872 | tf_op jit(solution)/shard_map/ppermute | solution.py:23
  13.5 0.0 copy-done.2
  13.5 0.0 copy-done.4
  13.5 0.0 copy-done.5
  13.5 0.0 copy-done.6
  13.5 0.0 copy-done.3
  13.5 0.0 copy-done
  13.5 0.0 copy-done.8
  13.5 0.0 copy-done.7
  13.5 0.0 copy-done.1
  13.5 8.6 %first_tick.2 = (bf16[2048,128]{1,0:T(8,128)(2,1)S(1)}, f32[6,128,128]{2,1,0:T(8,128)S(1)}, f32[16,128]{1,0:T(8,128)S(1)}, f32[3,128,128]{2,1,0:T(8,128)S(1)}, f32[128,128]{1,0:T(8,128)S(1)}) custom-call(bf16[1,2,1,4096,128]{4,3,2,1,0:T(8,128)(2,1)S(1)} %copy-done, bf16[4096,128]{1,0:T(8,128)(2,1)S(1)} %bitcast.7, f32[3,7,1,256]{3,2,1,0:T(1,128)S(1)} %bitcast.9, ...), custom_call_target="tpu_custom_call" | custom-call | tf_op jit(solution)/shard_map/first_tick/pallas_call | solution.py:375
  22.2 2.8 %collective-permute-start = (bf16[2048,128]{1,0:T(8,128)(2,1)S(1)}, bf16[2048,128]{1,0:T(8,128)(2,1)S(1)}, u32[]{:S(2)}, u32[]{:S(2)}) collective-permute-start(bf16[2048,128]{1,0:T(8,128)(2,1)S(1)} %get-tuple-element.16), channel_id=1, source_target_pairs={{4,0},{8,4},{12,8},{16,12},{20,16},{24,20},{28,24},{5,1},{9,5},{13... | collective-permute-start | bytes 1572872 | tf_op jit(solution)/shard_map/ppermute | solution.py:23
  24.9 0.0 collective-permute-done.1.refs_1_
  24.9 6.6 %last_tick.2.refs_12_ = bf16[176,128]{1,0:T(8,128)(2,1)S(1)} custom-call(bf16[1,2,1,4096,128]{4,3,2,1,0:T(8,128)(2,1)S(1)} %copy-done, bf16[2048,128]{1,0:T(8,128)(2,1)S(1)} %collective-permute-done.1.refs_1_, f32[3,7,1,256]{3,2,1,0:T(1,128)S(1)} %bitcast.10, f32[1,256,128]{2,1,0:T(8,128)S(1)} %copy-done.3, f32[32,128]{1,0:T(8,128)S(1)} %bitcast.14, ...), custom_call_target="tpu_custom_call" | custom-call | tf_op jit(solution)/shard_map/last_tick/pallas_call | solution.py:375
  31.6 0.0 collective-permute-done.refs_1_
  31.6 6.7 %last_tick.3.refs_0_ = bf16[352,128]{1,0:T(8,128)(2,1)S(1)} custom-call(bf16[1,2,1,4096,128]{4,3,2,1,0:T(8,128)(2,1)S(1)} %copy-done, bf16[2048,128]{1,0:T(8,128)(2,1)S(1)} %collective-permute-done.refs_1_, f32[3,7,1,256]{3,2,1,0:T(1,128)S(1)} %bitcast.11, f32[1,256,128]{2,1,0:T(8,128)S(1)} %copy-done.3, f32[32,128]{1,0:T(8,128)S(1)} %bitcast.15, ...), custom_call_target="tpu_custom_call" | custom-call | tf_op jit(solution)/shard_map/last_tick/pallas_call | solution.py:375
  38.3 3.6 %collective-permute-start.4 = (bf16[352,128]{1,0:T(8,128)(2,1)S(1)}, bf16[352,128]{1,0:T(8,128)(2,1)S(1)}, u32[]{:S(2)}, u32[]{:S(2)}) collective-permute-start(bf16[352,128]{1,0:T(8,128)(2,1)S(1)} %last_tick.3.refs_0_), channel_id=1, source_target_pairs={{0,3},{1,2},{2,1},{3,0},{4,7},{5,6},{6,5},{7,4},{8,11},{9,10},{10,... | collective-permute-start | bytes 270344 | tf_op jit(solution)/shard_map/ppermute | solution.py:448
  41.9 0.0 collective-permute-start.3
  41.9 0.8 %collective-permute-start.2 = (bf16[352,128]{1,0:T(8,128)(2,1)S(1)}, bf16[352,128]{1,0:T(8,128)(2,1)S(1)}, u32[]{:S(2)}, u32[]{:S(2)}) collective-permute-start(bf16[352,128]{1,0:T(8,128)(2,1)S(1)} %last_tick.3.refs_0_), channel_id=1, source_target_pairs={{0,1},{1,0},{2,3},{3,2},{4,5},{5,4},{6,7},{7,6},{8,9},{9,8},{10,11... | collective-permute-start | bytes 270344 | tf_op jit(solution)/shard_map/ppermute | solution.py:448
  42.7 3.0 %collective-permute-done.4.refs_3_ = bf16[352,128]{1,0:T(8,128)(2,1)S(1)} collective-permute-done((bf16[352,128]{1,0:T(8,128)(2,1)S(1)}, bf16[352,128]{1,0:T(8,128)(2,1)S(1)}, u32[]{:S(2)}, u32[]{:S(2)}) %collective-permute-start.4) | collective-permute-done | bytes 90144 | tf_op jit(solution)/shard_map/ppermute | solution.py:448
  45.7 4.6 %collective-permute-done.3.refs_2_ = bf16[352,128]{1,0:T(8,128)(2,1)S(1)} collective-permute-done((bf16[352,128]{1,0:T(8,128)(2,1)S(1)}, bf16[352,128]{1,0:T(8,128)(2,1)S(1)}, u32[]{:S(2)}, u32[]{:S(2)}) %collective-permute-start.3) | collective-permute-done | bytes 90144 | tf_op jit(solution)/shard_map/ppermute | solution.py:448
  50.3 0.0 collective-permute-done.2.refs_1_
  50.3 0.7 %finish.1 = (f32[3,7,1,256]{3,2,1,0:T(1,128)}, f32[256,128]{1,0:T(8,128)}, f32[32,128]{1,0:T(8,128)}) custom-call(bf16[352,128]{1,0:T(8,128)(2,1)S(1)} %last_tick.3.refs_0_, bf16[352,128]{1,0:T(8,128)(2,1)S(1)} %collective-permute-done.2.refs_1_, bf16[352,128]{1,0:T(8,128)(2,1)S(1)} %collective-permute-done.3.refs_2_, ...), custom_call_target="tpu_custom_call" | custom-call | tf_op jit(solution)/shard_map/finish/pallas_call | solution.py:417
Async XLA Ops:
  0.6 12.8 %copy-start.2 = (bf16[128,768]{1,0:T(8,128)(2,1)S(1)}, bf16[128,768]{1,0:T(8,128)(2,1)}, u32[]{:S(2)}) copy-start(bf16[128,768]{1,0:T(8,128)(2,1)} %constant.10.clone.refs_7_) | copy-start | bytes 589828
  0.6 12.8 %copy-start.4 = (bf16[256,256]{1,0:T(8,128)(2,1)S(1)}, bf16[256,256]{1,0:T(8,128)(2,1)}, u32[]{:S(2)}) copy-start(bf16[256,256]{1,0:T(8,128)(2,1)} %constant.9.clone.refs_6_) | copy-start | bytes 393220
  0.7 12.8 %copy-start.5 = (bf16[256,256]{1,0:T(8,128)(2,1)S(1)}, bf16[256,256]{1,0:T(8,128)(2,1)}, u32[]{:S(2)}) copy-start(bf16[256,256]{1,0:T(8,128)(2,1)} %constant.8.clone.refs_5_) | copy-start | bytes 393220
  0.7 12.8 %copy-start.6 = (bf16[768,128]{1,0:T(8,128)(2,1)S(1)}, bf16[768,128]{1,0:T(8,128)(2,1)}, u32[]{:S(2)}) copy-start(bf16[768,128]{1,0:T(8,128)(2,1)} %constant.11.clone.refs_8_) | copy-start | bytes 589828
  0.7 12.8 %copy-start.3 = (f32[1,256,128]{2,1,0:T(8,128)S(1)}, f32[1,256,128]{2,1,0:T(8,128)}, u32[]{:S(2)}) copy-start(f32[1,256,128]{2,1,0:T(8,128)} %refs_3_.7) | copy-start | bytes 393220
  0.7 12.8 %copy-start = (bf16[1,2,1,4096,128]{4,3,2,1,0:T(8,128)(2,1)S(1)}, bf16[1,2,1,4096,128]{4,3,2,1,0:T(8,128)(2,1)}, u32[]{:S(2)}) copy-start(bf16[1,2,1,4096,128]{4,3,2,1,0:T(8,128)(2,1)} %refs_0_.7) | copy-start | bytes 6291460
  0.7 12.8 %copy-start.8 = (f32[1,4096]{1,0:T(1,128)S(1)}, f32[1,4096]{1,0:T(1,128)}, u32[]{:S(2)}) copy-start(f32[1,4096]{1,0:T(1,128)} %param.13) | copy-start | bytes 49156
  0.7 12.8 %copy-start.7 = (f32[1,3,256,7]{2,0,3,1:T(1,128)S(1)}, f32[1,3,256,7]{2,0,3,1:T(1,128)}, u32[]{:S(2)}) copy-start(f32[1,3,256,7]{2,0,3,1:T(1,128)} %param.11) | copy-start | bytes 64516
  0.7 12.8 %copy-start.1 = (bf16[1,1,4096,128]{3,2,1,0:T(8,128)(2,1)S(1)}, bf16[1,1,4096,128]{3,2,1,0:T(8,128)(2,1)}, u32[]{:S(2)}) copy-start(bf16[1,1,4096,128]{3,2,1,0:T(8,128)(2,1)} %param.10) | copy-start | bytes 3145732
  10.7 14.3 %collective-permute-start.1 = (bf16[2048,128]{1,0:T(8,128)(2,1)S(1)}, bf16[2048,128]{1,0:T(8,128)(2,1)S(1)}, u32[]{:S(2)}, u32[]{:S(2)}) collective-permute-start(bf16[2048,128]{1,0:T(8,128)(2,1)S(1)} %get-tuple-element.21), channel_id=1, source_target_pairs={{4,0},{8,4},{12,8},{16,12},{20,16},{24,20},{28,24},{5,1},{9,5},{13... | collective-permute-start | bytes 1572872 | tf_op jit(solution)/shard_map/ppermute | solution.py:23
  22.2 9.4 %collective-permute-start = (bf16[2048,128]{1,0:T(8,128)(2,1)S(1)}, bf16[2048,128]{1,0:T(8,128)(2,1)S(1)}, u32[]{:S(2)}, u32[]{:S(2)}) collective-permute-start(bf16[2048,128]{1,0:T(8,128)(2,1)S(1)} %get-tuple-element.16), channel_id=1, source_target_pairs={{4,0},{8,4},{12,8},{16,12},{20,16},{24,20},{28,24},{5,1},{9,5},{13... | collective-permute-start | bytes 1572872 | tf_op jit(solution)/shard_map/ppermute | solution.py:23
  38.3 7.4 %collective-permute-start.4 = (bf16[352,128]{1,0:T(8,128)(2,1)S(1)}, bf16[352,128]{1,0:T(8,128)(2,1)S(1)}, u32[]{:S(2)}, u32[]{:S(2)}) collective-permute-start(bf16[352,128]{1,0:T(8,128)(2,1)S(1)} %last_tick.3.refs_0_), channel_id=1, source_target_pairs={{0,3},{1,2},{2,1},{3,0},{4,7},{5,6},{6,5},{7,4},{8,11},{9,10},{10,... | collective-permute-start | bytes 270344 | tf_op jit(solution)/shard_map/ppermute | solution.py:448
  41.9 8.4 %collective-permute-start.3 = (bf16[352,128]{1,0:T(8,128)(2,1)S(1)}, bf16[352,128]{1,0:T(8,128)(2,1)S(1)}, u32[]{:S(2)}, u32[]{:S(2)}) collective-permute-start(bf16[352,128]{1,0:T(8,128)(2,1)S(1)} %last_tick.3.refs_0_), channel_id=1, source_target_pairs={{0,2},{1,3},{2,0},{3,1},{4,6},{5,7},{6,4},{7,5},{8,10},{9,11},{10,... | collective-permute-start | bytes 270344 | tf_op jit(solution)/shard_map/ppermute | solution.py:448
  41.9 8.4 %collective-permute-start.2 = (bf16[352,128]{1,0:T(8,128)(2,1)S(1)}, bf16[352,128]{1,0:T(8,128)(2,1)S(1)}, u32[]{:S(2)}, u32[]{:S(2)}) collective-permute-start(bf16[352,128]{1,0:T(8,128)(2,1)S(1)} %last_tick.3.refs_0_), channel_id=1, source_target_pairs={{0,1},{1,0},{2,3},{3,2},{4,5},{5,4},{6,7},{7,6},{8,9},{9,8},{10,11... | collective-permute-start | bytes 270344 | tf_op jit(solution)/shard_map/ppermute | solution.py:448

commit v6 on v5

--- a/solution.py
+++ b/solution.py
@@ -254,7 +254,7 @@
                 step(RING * index + u, u, RING)
             return 0
 
-        lax.fori_loop(0, blocks // RING - 1, turn, 0)
+        lax.fori_loop(0, blocks // RING - 1, turn, 0, unroll=self.last)
         for u in range(RING):
             step(blocks - RING + u, u, RING - u)
         self.finish(blocks - 1, (blocks - 1) % RING)

time: 51.2 us -> 50.9 us (level)
  Pallas kernels: 32.6 us -> 31.6 us
    pallas_call x4, Pallas kernels: 31.9 us -> 30.9 us  [run_tick(): pl.pallas_call(functools.partial(tick_kernel, last, taps, (len(ins), len(...]
  transfers between devices with their start and end apart: 5 -> 5, of which waited for: 2 -> 3; matrix products, arithmetic and copies ran while one was open for 0% -> 0% of each run, Pallas kernels for 30% -> 29%
where the time goes in v6:
time: 50.9 us; the launch traced here: 50.6 us
  Pallas kernels  31.6 us (62%)
  starting transfers between devices  9.96 us (20%)
  waiting for transfers between devices  8.14 us (16%)
  between operations  0.8 us (2%)
    pallas_call x4, Pallas kernels, run_tick(): pl.pallas_call(functools.partial(tick_kernel, last, taps, (len(ins), len(...  30.9 us
    ppermute x3, waiting for transfers between devices, body(): parts.append(lax.ppermute(message[0], 'replica', pairs))  7.81 us
    ppermute x2, starting transfers between devices, shifted(): return lax.ppermute(array, axis, pairs)  5.55 us
    ppermute x3, starting transfers between devices, body(): parts.append(lax.ppermute(message[0], 'replica', pairs))  4.41 us
  transfers between devices with their start and end apart: 5, of which 3 were waited for; matrix products, arithmetic and copies ran while one was open for 0% of the time, Pallas kernels for 29%

profile of v6, /device:TPU:4, one launch (start us, length us, event | category | flops | bytes accessed | tf_op | source)
XLA Modules:
  0.0 50.6 jit_solution(2959571020796972677)
XLA Ops:
  0.6 0.0 copy-start.2
  0.6 0.0 copy-start.4
  0.7 0.0 copy-start.5
  0.7 0.0 copy-start.6
  0.7 0.0 copy-start.3
  0.7 0.0 copy-start
  0.7 0.0 copy-start.8
  0.7 0.0 copy-start.7
  0.7 0.0 copy-start.1
  0.7 9.9 %first_tick.3 = (bf16[2048,128]{1,0:T(8,128)(2,1)S(1)}, f32[6,128,128]{2,1,0:T(8,128)S(1)}, f32[16,128]{1,0:T(8,128)S(1)}, f32[3,128,128]{2,1,0:T(8,128)S(1)}, f32[128,128]{1,0:T(8,128)S(1)}) custom-call(bf16[1,2,1,4096,128]{4,3,2,1,0:T(8,128)(2,1)} %refs_0_.7, bf16[4096,128]{1,0:T(8,128)(2,1)} %bitcast.6, f32[3,7,1,256]{3,2,1,0:T(1,128)} %bitcast.8, ...), custom_call_target="tpu_custom_call" | custom-call | tf_op jit(solution)/shard_map/first_tick/pallas_call | solution.py:375
  10.7 2.8 %collective-permute-start.1 = (bf16[2048,128]{1,0:T(8,128)(2,1)S(1)}, bf16[2048,128]{1,0:T(8,128)(2,1)S(1)}, u32[]{:S(2)}, u32[]{:S(2)}) collective-permute-start(bf16[2048,128]{1,0:T(8,128)(2,1)S(1)} %get-tuple-element.21), channel_id=1, source_target_pairs={{4,0},{8,4},{12,8},{16,12},{20,16},{24,20},{28,24},{5,1},{9,5},{13... | collective-permute-start | bytes 1572872 | tf_op jit(solution)/shard_map/ppermute | solution.py:23
  13.5 0.0 copy-done.2
  13.5 0.0 copy-done.4
  13.5 0.0 copy-done.5
  13.5 0.0 copy-done.6
  13.5 0.0 copy-done.3
  13.5 0.0 copy-done
  13.5 0.0 copy-done.8
  13.5 0.0 copy-done.7
  13.5 0.0 copy-done.1
  13.5 8.6 %first_tick.2 = (bf16[2048,128]{1,0:T(8,128)(2,1)S(1)}, f32[6,128,128]{2,1,0:T(8,128)S(1)}, f32[16,128]{1,0:T(8,128)S(1)}, f32[3,128,128]{2,1,0:T(8,128)S(1)}, f32[128,128]{1,0:T(8,128)S(1)}) custom-call(bf16[1,2,1,4096,128]{4,3,2,1,0:T(8,128)(2,1)S(1)} %copy-done, bf16[4096,128]{1,0:T(8,128)(2,1)S(1)} %bitcast.7, f32[3,7,1,256]{3,2,1,0:T(1,128)S(1)} %bitcast.9, ...), custom_call_target="tpu_custom_call" | custom-call | tf_op jit(solution)/shard_map/first_tick/pallas_call | solution.py:375
  22.2 2.8 %collective-permute-start = (bf16[2048,128]{1,0:T(8,128)(2,1)S(1)}, bf16[2048,128]{1,0:T(8,128)(2,1)S(1)}, u32[]{:S(2)}, u32[]{:S(2)}) collective-permute-start(bf16[2048,128]{1,0:T(8,128)(2,1)S(1)} %get-tuple-element.16), channel_id=1, source_target_pairs={{4,0},{8,4},{12,8},{16,12},{20,16},{24,20},{28,24},{5,1},{9,5},{13... | collective-permute-start | bytes 1572872 | tf_op jit(solution)/shard_map/ppermute | solution.py:23
  24.9 0.0 collective-permute-done.1.refs_1_
  24.9 6.2 %last_tick.2.refs_12_ = bf16[176,128]{1,0:T(8,128)(2,1)S(1)} custom-call(bf16[1,2,1,4096,128]{4,3,2,1,0:T(8,128)(2,1)S(1)} %copy-done, bf16[2048,128]{1,0:T(8,128)(2,1)S(1)} %collective-permute-done.1.refs_1_, f32[3,7,1,256]{3,2,1,0:T(1,128)S(1)} %bitcast.10, f32[1,256,128]{2,1,0:T(8,128)S(1)} %copy-done.3, f32[32,128]{1,0:T(8,128)S(1)} %bitcast.14, ...), custom_call_target="tpu_custom_call" | custom-call | tf_op jit(solution)/shard_map/last_tick/pallas_call | solution.py:375
  31.1 0.3 collective-permute-done.refs_1_
  31.4 6.2 %last_tick.3.refs_0_ = bf16[352,128]{1,0:T(8,128)(2,1)S(1)} custom-call(bf16[1,2,1,4096,128]{4,3,2,1,0:T(8,128)(2,1)S(1)} %copy-done, bf16[2048,128]{1,0:T(8,128)(2,1)S(1)} %collective-permute-done.refs_1_, f32[3,7,1,256]{3,2,1,0:T(1,128)S(1)} %bitcast.11, f32[1,256,128]{2,1,0:T(8,128)S(1)} %copy-done.3, f32[32,128]{1,0:T(8,128)S(1)} %bitcast.15, ...), custom_call_target="tpu_custom_call" | custom-call | tf_op jit(solution)/shard_map/last_tick/pallas_call | solution.py:375
  37.7 3.6 %collective-permute-start.4 = (bf16[352,128]{1,0:T(8,128)(2,1)S(1)}, bf16[352,128]{1,0:T(8,128)(2,1)S(1)}, u32[]{:S(2)}, u32[]{:S(2)}) collective-permute-start(bf16[352,128]{1,0:T(8,128)(2,1)S(1)} %last_tick.3.refs_0_), channel_id=1, source_target_pairs={{0,3},{1,2},{2,1},{3,0},{4,7},{5,6},{6,5},{7,4},{8,11},{9,10},{10,... | collective-permute-start | bytes 270344 | tf_op jit(solution)/shard_map/ppermute | solution.py:448
  41.3 0.0 collective-permute-start.3
  41.3 0.8 %collective-permute-start.2 = (bf16[352,128]{1,0:T(8,128)(2,1)S(1)}, bf16[352,128]{1,0:T(8,128)(2,1)S(1)}, u32[]{:S(2)}, u32[]{:S(2)}) collective-permute-start(bf16[352,128]{1,0:T(8,128)(2,1)S(1)} %last_tick.3.refs_0_), channel_id=1, source_target_pairs={{0,1},{1,0},{2,3},{3,2},{4,5},{5,4},{6,7},{7,6},{8,9},{9,8},{10,11... | collective-permute-start | bytes 270344 | tf_op jit(solution)/shard_map/ppermute | solution.py:448
  42.1 3.0 %collective-permute-done.4.refs_3_ = bf16[352,128]{1,0:T(8,128)(2,1)S(1)} collective-permute-done((bf16[352,128]{1,0:T(8,128)(2,1)S(1)}, bf16[352,128]{1,0:T(8,128)(2,1)S(1)}, u32[]{:S(2)}, u32[]{:S(2)}) %collective-permute-start.4) | collective-permute-done | bytes 90144 | tf_op jit(solution)/shard_map/ppermute | solution.py:448
  45.1 4.8 %collective-permute-done.3.refs_2_ = bf16[352,128]{1,0:T(8,128)(2,1)S(1)} collective-permute-done((bf16[352,128]{1,0:T(8,128)(2,1)S(1)}, bf16[352,128]{1,0:T(8,128)(2,1)S(1)}, u32[]{:S(2)}, u32[]{:S(2)}) %collective-permute-start.3) | collective-permute-done | bytes 90144 | tf_op jit(solution)/shard_map/ppermute | solution.py:448
  49.9 0.0 collective-permute-done.2.refs_1_
  49.9 0.7 %finish.1 = (f32[3,7,1,256]{3,2,1,0:T(1,128)}, f32[256,128]{1,0:T(8,128)}, f32[32,128]{1,0:T(8,128)}) custom-call(bf16[352,128]{1,0:T(8,128)(2,1)S(1)} %last_tick.3.refs_0_, bf16[352,128]{1,0:T(8,128)(2,1)S(1)} %collective-permute-done.2.refs_1_, bf16[352,128]{1,0:T(8,128)(2,1)S(1)} %collective-permute-done.3.refs_2_, ...), custom_call_target="tpu_custom_call" | custom-call | tf_op jit(solution)/shard_map/finish/pallas_call | solution.py:417
Async XLA Ops:
  0.6 12.8 %copy-start.2 = (bf16[128,768]{1,0:T(8,128)(2,1)S(1)}, bf16[128,768]{1,0:T(8,128)(2,1)}, u32[]{:S(2)}) copy-start(bf16[128,768]{1,0:T(8,128)(2,1)} %constant.10.clone.refs_7_) | copy-start | bytes 589828
  0.6 12.8 %copy-start.4 = (bf16[256,256]{1,0:T(8,128)(2,1)S(1)}, bf16[256,256]{1,0:T(8,128)(2,1)}, u32[]{:S(2)}) copy-start(bf16[256,256]{1,0:T(8,128)(2,1)} %constant.9.clone.refs_6_) | copy-start | bytes 393220
  0.7 12.8 %copy-start.5 = (bf16[256,256]{1,0:T(8,128)(2,1)S(1)}, bf16[256,256]{1,0:T(8,128)(2,1)}, u32[]{:S(2)}) copy-start(bf16[256,256]{1,0:T(8,128)(2,1)} %constant.8.clone.refs_5_) | copy-start | bytes 393220
  0.7 12.8 %copy-start.6 = (bf16[768,128]{1,0:T(8,128)(2,1)S(1)}, bf16[768,128]{1,0:T(8,128)(2,1)}, u32[]{:S(2)}) copy-start(bf16[768,128]{1,0:T(8,128)(2,1)} %constant.11.clone.refs_8_) | copy-start | bytes 589828
  0.7 12.8 %copy-start.3 = (f32[1,256,128]{2,1,0:T(8,128)S(1)}, f32[1,256,128]{2,1,0:T(8,128)}, u32[]{:S(2)}) copy-start(f32[1,256,128]{2,1,0:T(8,128)} %refs_3_.7) | copy-start | bytes 393220
  0.7 12.8 %copy-start = (bf16[1,2,1,4096,128]{4,3,2,1,0:T(8,128)(2,1)S(1)}, bf16[1,2,1,4096,128]{4,3,2,1,0:T(8,128)(2,1)}, u32[]{:S(2)}) copy-start(bf16[1,2,1,4096,128]{4,3,2,1,0:T(8,128)(2,1)} %refs_0_.7) | copy-start | bytes 6291460
  0.7 12.8 %copy-start.8 = (f32[1,4096]{1,0:T(1,128)S(1)}, f32[1,4096]{1,0:T(1,128)}, u32[]{:S(2)}) copy-start(f32[1,4096]{1,0:T(1,128)} %param.13) | copy-start | bytes 49156
  0.7 12.8 %copy-start.7 = (f32[1,3,256,7]{2,0,3,1:T(1,128)S(1)}, f32[1,3,256,7]{2,0,3,1:T(1,128)}, u32[]{:S(2)}) copy-start(f32[1,3,256,7]{2,0,3,1:T(1,128)} %param.11) | copy-start | bytes 64516
  0.7 12.8 %copy-start.1 = (bf16[1,1,4096,128]{3,2,1,0:T(8,128)(2,1)S(1)}, bf16[1,1,4096,128]{3,2,1,0:T(8,128)(2,1)}, u32[]{:S(2)}) copy-start(bf16[1,1,4096,128]{3,2,1,0:T(8,128)(2,1)} %param.10) | copy-start | bytes 3145732
  10.7 14.3 %collective-permute-start.1 = (bf16[2048,128]{1,0:T(8,128)(2,1)S(1)}, bf16[2048,128]{1,0:T(8,128)(2,1)S(1)}, u32[]{:S(2)}, u32[]{:S(2)}) collective-permute-start(bf16[2048,128]{1,0:T(8,128)(2,1)S(1)} %get-tuple-element.21), channel_id=1, source_target_pairs={{4,0},{8,4},{12,8},{16,12},{20,16},{24,20},{28,24},{5,1},{9,5},{13... | collective-permute-start | bytes 1572872 | tf_op jit(solution)/shard_map/ppermute | solution.py:23
  22.2 9.3 %collective-permute-start = (bf16[2048,128]{1,0:T(8,128)(2,1)S(1)}, bf16[2048,128]{1,0:T(8,128)(2,1)S(1)}, u32[]{:S(2)}, u32[]{:S(2)}) collective-permute-start(bf16[2048,128]{1,0:T(8,128)(2,1)S(1)} %get-tuple-element.16), channel_id=1, source_target_pairs={{4,0},{8,4},{12,8},{16,12},{20,16},{24,20},{28,24},{5,1},{9,5},{13... | collective-permute-start | bytes 1572872 | tf_op jit(solution)/shard_map/ppermute | solution.py:23
  37.7 7.4 %collective-permute-start.4 = (bf16[352,128]{1,0:T(8,128)(2,1)S(1)}, bf16[352,128]{1,0:T(8,128)(2,1)S(1)}, u32[]{:S(2)}, u32[]{:S(2)}) collective-permute-start(bf16[352,128]{1,0:T(8,128)(2,1)S(1)} %last_tick.3.refs_0_), channel_id=1, source_target_pairs={{0,3},{1,2},{2,1},{3,0},{4,7},{5,6},{6,5},{7,4},{8,11},{9,10},{10,... | collective-permute-start | bytes 270344 | tf_op jit(solution)/shard_map/ppermute | solution.py:448
  41.3 8.6 %collective-permute-start.3 = (bf16[352,128]{1,0:T(8,128)(2,1)S(1)}, bf16[352,128]{1,0:T(8,128)(2,1)S(1)}, u32[]{:S(2)}, u32[]{:S(2)}) collective-permute-start(bf16[352,128]{1,0:T(8,128)(2,1)S(1)} %last_tick.3.refs_0_), channel_id=1, source_target_pairs={{0,2},{1,3},{2,0},{3,1},{4,6},{5,7},{6,4},{7,5},{8,10},{9,11},{10,... | collective-permute-start | bytes 270344 | tf_op jit(solution)/shard_map/ppermute | solution.py:448
  41.3 8.6 %collective-permute-start.2 = (bf16[352,128]{1,0:T(8,128)(2,1)S(1)}, bf16[352,128]{1,0:T(8,128)(2,1)S(1)}, u32[]{:S(2)}, u32[]{:S(2)}) collective-permute-start(bf16[352,128]{1,0:T(8,128)(2,1)S(1)} %last_tick.3.refs_0_), channel_id=1, source_target_pairs={{0,1},{1,0},{2,3},{3,2},{4,5},{5,4},{6,7},{7,6},{8,9},{9,8},{10,11... | collective-permute-start | bytes 270344 | tf_op jit(solution)/shard_map/ppermute | solution.py:448
